TPU v7x, 32 devices: a whole 2x2x4 slice. The times are simulated.
32 devices in a mesh: dp: 4 (over z), row: 2 (over y), col: 4 (over x, core).
Axes of the slice: x: 2, y: 2, z: 4, core: 2. Of those that a mesh axis runs over, the one named last changes fastest.
Arguments:
- hidden_in: bfloat16 [1024, 2048], P('dp', ('row', 'col')), may hold values from -6 to 6
- seq_lengths: int32 [4], P('dp'), may hold values from 128 to 256, as said below
- query_weight: bfloat16 [2048, 2048], P('row', 'col'), may hold values from -0.8838835 to 0.8838835
- key_weight: bfloat16 [2048, 2048], P('row', 'col'), may hold values from -0.8838835 to 0.8838835
- value_weight: bfloat16 [2048, 2048], P('row', 'col'), may hold values from -0.125 to 0.125
- output_weight: bfloat16 [2048, 2048], P('col', 'row'), may hold values from -0.125 to 0.125
- gate_weight: bfloat16 [2048, 8192], P('row', 'col'), may hold values from -0.125 to 0.125
- up_weight: bfloat16 [2048, 8192], P('row', 'col'), may hold values from -0.125 to 0.125
- down_weight: bfloat16 [8192, 2048], P('col', 'row'), may hold values from -0.0625 to 0.0625
- query_gain: float32 [2048], replicated, may hold values from 0.5 to 5
- key_gain: float32 [2048], replicated, may hold values from 0.5 to 5
- mixer_gain: float32 [2048], replicated, may hold values from 0.1 to 1.9
- feed_gain: float32 [2048], replicated, may hold values from 0.1 to 1.9
- out_grad: bfloat16 [1024, 2048], P('dp', ('row', 'col')), may hold values from -6 to 6
Outputs:
- block_out: bfloat16 [1024, 2048], P('dp', ('row', 'col'))
- input_grad: bfloat16 [1024, 2048], P('dp', ('row', 'col'))
- query_weight_grad: float32 [2048, 2048], P(('row', 'dp'), 'col')
- key_weight_grad: float32 [2048, 2048], P(('row', 'dp'), 'col')
- value_weight_grad: float32 [2048, 2048], P(('row', 'dp'), 'col')
- output_weight_grad: float32 [2048, 2048], P(('col', 'dp'), 'row')
- gate_weight_grad: float32 [2048, 8192], P(('row', 'dp'), 'col')
- up_weight_grad: float32 [2048, 8192], P(('row', 'dp'), 'col')
- down_weight_grad: float32 [8192, 2048], P(('col', 'dp'), 'row')
- query_gain_grad: float32 [2048], replicated
- key_gain_grad: float32 [2048], replicated
- mixer_gain_grad: float32 [2048], replicated
- feed_gain_grad: float32 [2048], replicated
Inputs may be any that keep to these rules, and one draw needn't show every extreme that they name: `seq_lengths`: each index of dp holds one sequence in its first slots; the other slots are padding.
All inputs are finite; a program needn't handle non-finite values.
Results may differ from a plain program's by a relative error of at most 0.015.
Values may be sent and summed in bfloat16 or wider, within the bound.
No kernel may reach another device: no remote copies, remote signals or barrier semaphores. Data moves between devices by JAX's collectives and lax.ppermute only.
A program may use at most 192 MiB of HBM per device.

v0:
```python
import jax
import jax.numpy as jnp
from jax import lax
from jax.sharding import PartitionSpec as P

D = 2048
HD = 128


epsilon = 1e-06
rope_base = 500000.0


def widen(tensor):
    return lax.all_gather(tensor, "col", axis=1, tiled=True)


def row_whole(tensor):
    return lax.all_gather(tensor, "row", axis=1, tiled=True)


def col_share(tensor):
    return lax.psum_scatter(tensor, "col", scatter_dimension=1, tiled=True)


def row_back(tensor):
    return lax.psum_scatter(tensor, "row", scatter_dimension=1, tiled=True)


def norm_total(tensor):
    return lax.psum(tensor, ("row", "col"))


def pair_total(first_sum, second_sum):
    return lax.psum((first_sum, second_sum), ("row", "col"))


def across_rows(left, right):
    return lax.dot_general(
        left, right, (((0,), (0,)), ((), ())), preferred_element_type=jnp.float32
    )


def against_cols(left, right):
    return lax.dot_general(
        left, right, (((1,), (1,)), ((), ())), preferred_element_type=jnp.float32
    )


def rope_tables(row_count):
    positions = jnp.arange(row_count, dtype=jnp.float32)
    rates = rope_base ** (-2.0 * jnp.arange(HD // 2, dtype=jnp.float32) / HD)
    angles = positions[:, None] * rates[None, :]
    return (jnp.cos(angles)[:, None, :], jnp.sin(angles)[:, None, :])


def rotate(tensor, cosine, sine):
    half_dim = tensor.shape[-1] // 2
    first_half = tensor[..., :half_dim]
    second_half = tensor[..., half_dim:]
    return jnp.concatenate(
        [first_half * cosine - second_half * sine, second_half * cosine + first_half * sine], -1
    )


def allowed_mask(first_row, last_row, seq_length):
    query_pos = jnp.arange(first_row, last_row)[:, None]
    key_pos = jnp.arange(last_row)[None, :]
    return ((key_pos <= query_pos) & (key_pos < seq_length))[None]


def block_scores(queries, keys, first_row, last_row, seq_length):
    scores = jnp.einsum("qhd,khd->hqk", queries, keys, preferred_element_type=jnp.float32) * HD ** (
        -0.5
    )
    return jnp.where(allowed_mask(first_row, last_row, seq_length), scores, -1e30)


def attend_forward(queries, keys, values, seq_length, block_rows):
    scores = block_scores(queries, keys, 0, block_rows, seq_length)
    row_max = jnp.max(scores, axis=-1, keepdims=True)
    exponent = jnp.exp(scores - row_max)
    denominator = jnp.sum(exponent, axis=-1, keepdims=True)
    probability = (exponent / denominator).astype(jnp.bfloat16)
    outputs = jnp.einsum("hqk,khd->qhd", probability, values, preferred_element_type=jnp.float32)
    log_parts = (row_max + jnp.log(denominator))[..., 0]
    return (outputs, log_parts)


def attend_backward(queries, keys, values, grad_attended, log_totals, seq_length, block_rows):
    score_scale = HD ** (-0.5)
    grad_keys = jnp.zeros(keys.shape, jnp.float32)
    grad_values = jnp.zeros(values.shape, jnp.float32)
    scores = block_scores(queries, keys, 0, block_rows, seq_length)
    probability = jnp.exp(scores - log_totals[:, 0:block_rows, None])
    grad_prob = jnp.einsum(
        "qhd,khd->hqk", grad_attended, values, preferred_element_type=jnp.float32
    )
    centre = jnp.sum(probability * grad_prob, axis=-1, keepdims=True)
    grad_scores = (probability * (grad_prob - centre)).astype(jnp.bfloat16)
    grad_queries = (
        jnp.einsum("hqk,khd->qhd", grad_scores, keys, preferred_element_type=jnp.float32)
        * score_scale
    )
    grad_keys = grad_keys.at[:block_rows].add(
        jnp.einsum("hqk,qhd->khd", grad_scores, queries, preferred_element_type=jnp.float32)
        * score_scale
    )
    grad_values = grad_values.at[:block_rows].add(
        jnp.einsum(
            "hqk,qhd->khd",
            probability.astype(jnp.bfloat16),
            grad_attended,
            preferred_element_type=jnp.float32,
        )
    )
    return (grad_queries, grad_keys, grad_values)


def norm_backward(grad_norm, source, scale_rows, gain_part, stat_sum):
    weighted = grad_norm * gain_part
    return scale_rows * weighted - source * scale_rows**3 * stat_sum[:, None] / D


def place_gain(term, offset):
    return lax.dynamic_update_slice_in_dim(jnp.zeros((D,), jnp.float32), term, offset, 0)


def body(
    hidden_in,
    seq_lengths,
    query_weight,
    key_weight,
    value_weight,
    output_weight,
    gate_weight,
    up_weight,
    down_weight,
    query_gain,
    key_gain,
    mixer_gain,
    feed_gain,
    out_grad,
):
    row_count = hidden_in.shape[0]
    local_width = hidden_in.shape[1]
    head_count = local_width // HD
    block_rows = min(512, row_count)
    row_place = lax.axis_index("row")
    col_place = lax.axis_index("col")
    feature_start = (row_place * lax.axis_size("col") + col_place) * local_width
    head_start = (col_place * lax.axis_size("row") + row_place) * local_width
    query_gain_part = lax.dynamic_slice_in_dim(query_gain, head_start, local_width)
    key_gain_part = lax.dynamic_slice_in_dim(key_gain, head_start, local_width)
    mixer_gain_part = lax.dynamic_slice_in_dim(mixer_gain, feature_start, local_width)
    feed_gain_part = lax.dynamic_slice_in_dim(feed_gain, feature_start, local_width)
    seq_length = seq_lengths[0]
    cosine, sine = rope_tables(row_count)
    shaped = (row_count, head_count, HD)
    input_block = widen(hidden_in)
    query_part = jnp.dot(input_block, query_weight, preferred_element_type=jnp.float32)
    key_part = jnp.dot(input_block, key_weight, preferred_element_type=jnp.float32)
    value_part = jnp.dot(input_block, value_weight, preferred_element_type=jnp.float32)
    query, key_proj, value_proj = (
        lax.psum_scatter(query_part, "row", scatter_dimension=1, tiled=True),
        lax.psum_scatter(key_part, "row", scatter_dimension=1, tiled=True),
        lax.psum_scatter(value_part, "row", scatter_dimension=1, tiled=True),
    )
    query_sq, key_sq = pair_total(jnp.sum(query * query, 1), jnp.sum(key_proj * key_proj, 1))
    query_scale = lax.rsqrt(query_sq / D + epsilon)[:, None]
    key_scale = lax.rsqrt(key_sq / D + epsilon)[:, None]
    query_rot = rotate(
        (query * query_scale * query_gain_part).reshape(shaped), cosine, sine
    ).astype(jnp.bfloat16)
    key_rot = rotate((key_proj * key_scale * key_gain_part).reshape(shaped), cosine, sine).astype(
        jnp.bfloat16
    )
    value_low = value_proj.reshape(shaped).astype(jnp.bfloat16)
    attended, log_totals = attend_forward(query_rot, key_rot, value_low, seq_length, block_rows)
    attended_low = attended.reshape(row_count, local_width).astype(jnp.bfloat16)
    attended_rows = row_whole(attended_low)
    mixer_out = col_share(jnp.dot(attended_rows, output_weight, preferred_element_type=jnp.float32))
    mixer_scale = lax.rsqrt(norm_total(jnp.sum(mixer_out * mixer_out, 1)) / D + epsilon)[:, None]
    residual = hidden_in.astype(jnp.float32) + mixer_out * mixer_scale * mixer_gain_part
    residual_block = widen(residual.astype(jnp.bfloat16))
    gate_part = jnp.dot(residual_block, gate_weight, preferred_element_type=jnp.float32)
    up_part = jnp.dot(residual_block, up_weight, preferred_element_type=jnp.float32)
    gate_val, up_val = (
        lax.psum_scatter(gate_part, "row", scatter_dimension=1, tiled=True),
        lax.psum_scatter(up_part, "row", scatter_dimension=1, tiled=True),
    )
    sigmoid_val = jax.nn.sigmoid(gate_val)
    activated = gate_val * sigmoid_val
    hidden_low = (activated * up_val).astype(jnp.bfloat16)
    hidden_rows = row_whole(hidden_low)
    feed_out = col_share(jnp.dot(hidden_rows, down_weight, preferred_element_type=jnp.float32))
    feed_scale = lax.rsqrt(norm_total(jnp.sum(feed_out * feed_out, 1)) / D + epsilon)[:, None]
    block_out = (residual + feed_out * feed_scale * feed_gain_part).astype(jnp.bfloat16)
    valid = (jnp.arange(row_count) < seq_length)[:, None]
    grad_out = jnp.where(valid, out_grad.astype(jnp.float32), 0.0)
    feed_gain_term = jnp.sum(grad_out * feed_out * feed_scale, 0)
    feed_stat = norm_total(jnp.sum(grad_out * feed_gain_part * feed_out, 1))
    grad_feed = norm_backward(grad_out, feed_out, feed_scale, feed_gain_part, feed_stat)
    grad_feed_block = widen(grad_feed.astype(jnp.bfloat16))
    down_grad_w = across_rows(hidden_rows, grad_feed_block)
    grad_hidden = row_back(against_cols(grad_feed_block, down_weight))
    grad_gate = (
        grad_hidden * up_val * sigmoid_val * (1.0 + gate_val * (1.0 - sigmoid_val))
    ).astype(jnp.bfloat16)
    grad_up = (grad_hidden * activated).astype(jnp.bfloat16)
    gate_rows, up_rows = (
        lax.all_gather(grad_gate, "row", axis=1, tiled=True),
        lax.all_gather(grad_up, "row", axis=1, tiled=True),
    )
    gate_grad_w = across_rows(residual_block, gate_rows)
    up_grad_w = across_rows(residual_block, up_rows)
    grad_residual = grad_out + col_share(
        against_cols(gate_rows, gate_weight) + against_cols(up_rows, up_weight)
    )
    mixer_gain_term = jnp.sum(grad_residual * mixer_out * mixer_scale, 0)
    mixer_stat = norm_total(jnp.sum(grad_residual * mixer_gain_part * mixer_out, 1))
    grad_mixer = norm_backward(grad_residual, mixer_out, mixer_scale, mixer_gain_part, mixer_stat)
    grad_mixer_block = widen(grad_mixer.astype(jnp.bfloat16))
    output_grad_w = across_rows(attended_rows, grad_mixer_block)
    grad_attended = row_back(against_cols(grad_mixer_block, output_weight)).astype(jnp.bfloat16)
    grad_query_rot, grad_key_rot, grad_value = attend_backward(
        query_rot,
        key_rot,
        value_low,
        grad_attended.reshape(shaped),
        log_totals,
        seq_length,
        block_rows,
    )
    grad_query_norm = rotate(grad_query_rot, cosine, -sine).reshape(row_count, local_width)
    grad_key_norm = rotate(grad_key_rot, cosine, -sine).reshape(row_count, local_width)
    query_gain_term = jnp.sum(grad_query_norm * query * query_scale, 0)
    key_gain_term = jnp.sum(grad_key_norm * key_proj * key_scale, 0)
    query_stat, key_stat = pair_total(
        jnp.sum(grad_query_norm * query_gain_part * query, 1),
        jnp.sum(grad_key_norm * key_gain_part * key_proj, 1),
    )
    grad_query = norm_backward(
        grad_query_norm, query, query_scale, query_gain_part, query_stat
    ).astype(jnp.bfloat16)
    grad_key = norm_backward(grad_key_norm, key_proj, key_scale, key_gain_part, key_stat).astype(
        jnp.bfloat16
    )
    grad_value_low = grad_value.reshape(row_count, local_width).astype(jnp.bfloat16)
    query_rows, key_rows, value_rows = (
        lax.all_gather(grad_query, "row", axis=1, tiled=True),
        lax.all_gather(grad_key, "row", axis=1, tiled=True),
        lax.all_gather(grad_value_low, "row", axis=1, tiled=True),
    )
    query_grad_w = across_rows(input_block, query_rows)
    key_grad_w = across_rows(input_block, key_rows)
    value_grad_w = across_rows(input_block, value_rows)
    grad_input = grad_residual + col_share(
        against_cols(query_rows, query_weight)
        + against_cols(key_rows, key_weight)
        + against_cols(value_rows, value_weight)
    )
    query_sum, key_sum, value_sum, output_sum, gate_sum, up_sum, down_sum = (
        lax.psum_scatter(query_grad_w, "dp", scatter_dimension=0, tiled=True),
        lax.psum_scatter(key_grad_w, "dp", scatter_dimension=0, tiled=True),
        lax.psum_scatter(value_grad_w, "dp", scatter_dimension=0, tiled=True),
        lax.psum_scatter(output_grad_w, "dp", scatter_dimension=0, tiled=True),
        lax.psum_scatter(gate_grad_w, "dp", scatter_dimension=0, tiled=True),
        lax.psum_scatter(up_grad_w, "dp", scatter_dimension=0, tiled=True),
        lax.psum_scatter(down_grad_w, "dp", scatter_dimension=0, tiled=True),
    )
    query_gain_sum, key_gain_sum, mixer_gain_sum, feed_gain_sum = lax.psum(
        (
            place_gain(query_gain_term, head_start),
            place_gain(key_gain_term, head_start),
            place_gain(mixer_gain_term, feature_start),
            place_gain(feed_gain_term, feature_start),
        ),
        ("dp", "row", "col"),
    )
    return (
        block_out,
        grad_input.astype(jnp.bfloat16),
        query_sum,
        key_sum,
        value_sum,
        output_sum,
        gate_sum,
        up_sum,
        down_sum,
        query_gain_sum,
        key_gain_sum,
        mixer_gain_sum,
        feed_gain_sum,
    )


def solution(mesh):
    in_specs = (
        P("dp", ("row", "col")),
        P("dp"),
        P("row", "col"),
        P("row", "col"),
        P("row", "col"),
        P("col", "row"),
        P("row", "col"),
        P("row", "col"),
        P("col", "row"),
        P(),
        P(),
        P(),
        P(),
        P("dp", ("row", "col")),
    )
    out_specs = (
        P("dp", ("row", "col")),
        P("dp", ("row", "col")),
        P(("row", "dp"), "col"),
        P(("row", "dp"), "col"),
        P(("row", "dp"), "col"),
        P(("col", "dp"), "row"),
        P(("row", "dp"), "col"),
        P(("row", "dp"), "col"),
        P(("col", "dp"), "row"),
        P(),
        P(),
        P(),
        P(),
    )
    return jax.shard_map(body, mesh=mesh, in_specs=in_specs, out_specs=out_specs, check_vma=False)
```

profile of v0, /device:TPU:0, one launch (start us, length us, event | category | flops | bytes accessed | tf_op | source)
XLA Modules:
  0.0 1144.3 jit_solution(4367425455699044301)
XLA Ops:
  7.3 9.0 all_gather.33
  16.2 2.5 fusion.32
  18.8 2.5 fusion.31
  26.1 8.2 reduce-scatter.23.cloned.1.call-done
  35.4 16.4 %reduce-scatter.21.cloned.1.call-done = f32[256,256]{1,0:T(8,128)} async-done(((f32[256,512]{1,0:T(8,128)}), f32[256,256]{1,0:T(8,128)}) %reduce-scatter.21.cloned.1.call-update) | async-done | bytes 262160 | tf_op jit(solution)/shard_map/reduce_scatter | solution.py:165
  52.9 12.7 %all-reduce.2 = (f32[256]{0:T(256)S(1)}, f32[256]{0:T(256)S(1)}) all-reduce(f32[256]{0:T(256)S(1)} %multiply_reduce_fusion.9, f32[256]{0:T(256)S(1)} %multiply_reduce_fusion.10), channel_id=1, replica_groups=mesh['dp'=4,'row'=2,'col'=4] {'row','col'}, use_global_device_ids=true, to_apply=%region_6.0 | all-reduce | flops 512 | bytes 4096 | tf_op jit(solution)/shard_map/psum | solution.py:35
  71.2 5.6 all_gather.34
  79.2 24.1 %reduce-scatter.25.cloned.1.call-done = f32[256,256]{1,0:T(8,128)} async-done(((f32[256,1024]{1,0:T(8,128)}), f32[256,256]{1,0:T(8,128)}) %reduce-scatter.25.cloned.1.call-update) | async-done | bytes 262160 | tf_op jit(solution)/shard_map/reduce_scatter | solution.py:23
  104.4 12.5 %psum.86 = f32[256]{0:T(256)S(1)} all-reduce(f32[256]{0:T(256)S(1)} %multiply_reduce_fusion.8), channel_id=1, replica_groups=mesh['dp'=4,'row'=2,'col'=4] {'row','col'}, use_global_device_ids=true, to_apply=%region_11.12 | all-reduce | flops 256 | bytes 2048 | tf_op jit(solution)/shard_map/psum | solution.py:31
  118.6 6.5 all_gather.35
  125.1 4.8 fusion.35
  129.9 4.8 fusion.34
  134.7 27.1 %reduce-scatter.29.cloned.1.call-done = f32[256,1024]{1,0:T(8,128)} async-done(((f32[256,2048]{1,0:T(8,128)}), f32[256,1024]{1,0:T(8,128)}) %reduce-scatter.29.cloned.1.call-update) | async-done | bytes 1048592 | tf_op jit(solution)/shard_map/reduce_scatter | solution.py:190
  161.8 34.6 %reduce-scatter.27.cloned.1.call-done = f32[256,1024]{1,0:T(8,128)} async-done(((f32[256,2048]{1,0:T(8,128)}), f32[256,1024]{1,0:T(8,128)}) %reduce-scatter.27.cloned.1.call-update) | async-done | bytes 1048592 | tf_op jit(solution)/shard_map/reduce_scatter | solution.py:189
  196.4 2.6 multiply_convert_fusion.2
  199.2 21.4 %all-gather.4.cloned.1.call-done = bf16[256,2048]{1,0:T(8,128)(2,1)} async-done(((bf16[256,1024]{1,0:T(8,128)(2,1)}), bf16[256,2048]{1,0:T(8,128)(2,1)}) %all-gather.4.cloned.1.call-update) | async-done | bytes 1048592 | tf_op jit(solution)/shard_map/all_gather | solution.py:19
  220.6 4.7 fusion.36
  226.1 24.1 %reduce-scatter.31.cloned.1.call-done = f32[256,256]{1,0:T(8,128)} async-done(((f32[256,1024]{1,0:T(8,128)}), f32[256,256]{1,0:T(8,128)}) %reduce-scatter.31.cloned.1.call-update) | async-done | bytes 262160 | tf_op jit(solution)/shard_map/reduce_scatter | solution.py:23
  251.3 12.5 %psum.87 = f32[256]{0:T(256)S(1)} all-reduce(f32[256]{0:T(256)S(1)} %multiply_reduce_fusion.7), channel_id=1, replica_groups=mesh['dp'=4,'row'=2,'col'=4] {'row','col'}, use_global_device_ids=true, to_apply=%region_16.17 | all-reduce | flops 256 | bytes 2048 | tf_op jit(solution)/shard_map/psum | solution.py:31
  265.6 11.8 %psum.88 = f32[256]{0:T(256)S(1)} all-reduce(f32[256]{0:T(256)S(1)} %get-tuple-element.73), channel_id=1, replica_groups=mesh['dp'=4,'row'=2,'col'=4] {'row','col'}, use_global_device_ids=true, to_apply=%region_18.19 | all-reduce | flops 256 | bytes 2048 | tf_op jit(solution)/shard_map/psum | solution.py:31
  278.5 6.8 all_gather.37
  285.3 5.0 fusion.37
  290.4 31.6 %reduce-scatter.33.cloned.1.call-done = f32[256,1024]{1,0:T(8,128)} async-done(((f32[256,2048]{1,0:T(8,128)}), f32[256,1024]{1,0:T(8,128)}) %reduce-scatter.33.cloned.1.call-update) | async-done | bytes 1048592 | tf_op jit(solution)/shard_map/reduce_scatter | solution.py:27
  322.0 3.5 multiply_convert_fusion
  326.5 20.5 %all-gather.6.cloned.1.call-done = bf16[256,2048]{1,0:T(8,128)(2,1)} async-done(((bf16[256,1024]{1,0:T(8,128)(2,1)}), bf16[256,2048]{1,0:T(8,128)(2,1)}) %all-gather.6.cloned.1.call-update) | async-done | bytes 1048592 | tf_op jit(solution)/shard_map/all_gather | solution.py:212
  346.9 4.8 fusion.38
  351.7 18.7 %all-gather.8.cloned.1.call-done = bf16[256,2048]{1,0:T(8,128)(2,1)} async-done(((bf16[256,1024]{1,0:T(8,128)(2,1)}), bf16[256,2048]{1,0:T(8,128)(2,1)}) %all-gather.8.cloned.1.call-update) | async-done | bytes 1048592 | tf_op jit(solution)/shard_map/all_gather | solution.py:213
  370.4 5.0 convolution_add_fusion.2
  375.5 24.9 %reduce-scatter.35.cloned.1.call-done = f32[256,256]{1,0:T(8,128)} async-done(((f32[256,1024]{1,0:T(8,128)}), f32[256,256]{1,0:T(8,128)}) %reduce-scatter.35.cloned.1.call-update) | async-done | bytes 262160 | tf_op jit(solution)/shard_map/reduce_scatter | solution.py:23
  402.1 13.2 %psum.89 = f32[256]{0:T(256)} all-reduce(f32[256]{0:T(256)} %get-tuple-element.67), channel_id=1, replica_groups=mesh['dp'=4,'row'=2,'col'=4] {'row','col'}, use_global_device_ids=true, to_apply=%region_22.23 | all-reduce | flops 256 | bytes 2048 | tf_op jit(solution)/shard_map/psum | solution.py:31
  417.2 6.5 all_gather.40
  425.8 13.9 %reduce-scatter.37.cloned.1.call-done = f32[256,256]{1,0:T(8,128)} async-done(((f32[256,512]{1,0:T(8,128)}), f32[256,256]{1,0:T(8,128)}) %reduce-scatter.37.cloned.1.call-update) | async-done | bytes 262160 | tf_op jit(solution)/shard_map/reduce_scatter | solution.py:27
  449.1 13.2 %all-reduce.1 = (f32[256]{0:T(256)}, f32[256]{0:T(256)}) all-reduce(f32[256]{0:T(256)} %get-tuple-element.71, f32[256]{0:T(256)} %get-tuple-element.69), channel_id=1, replica_groups=mesh['dp'=4,'row'=2,'col'=4] {'row','col'}, use_global_device_ids=true, to_apply=%region_26.27 | all-reduce | flops 512 | bytes 4096 | tf_op jit(solution)/shard_map/psum | solution.py:35
  463.4 5.6 all_gather.41
  471.7 5.6 all_gather.42
  477.3 6.1 all_gather.43
  494.1 4.5 fusion.44
  499.9 4.5 fusion.42
  505.6 4.5 fusion.43
  511.8 43.6 %all-reduce = (f32[2048]{0:T(1024)}, f32[2048]{0:T(1024)}, f32[2048]{0:T(1024)}, f32[2048]{0:T(1024)}) all-reduce(f32[2048]{0:T(1024)S(1)} %dynamic_update_slice.12, f32[2048]{0:T(1024)S(1)} %dynamic_update_slice.13, f32[2048]{0:T(1024)S(1)} %dynamic_update_slice.14, ...), channel_id=1, replica_groups=mesh['dp'=4,'row'=2,'col'=4] {'dp','row','col'}, use_global_device_ids=true, to_apply=%region_38.39 | all-reduce | flops 8192 | bytes 65536 | tf_op jit(solution)/shard_map/psum | solution.py:272
  558.8 2.0 copy.45
  560.9 43.0 %reduce-scatter.43.cloned.1.call-done = f32[256,512]{0,1:T(8,128)} async-done(((f32[1024,512]{0,1:T(8,128)}), f32[256,512]{0,1:T(8,128)}) %reduce-scatter.43.cloned.1.call-update) | async-done | bytes 524304 | tf_op jit(solution)/shard_map/reduce_scatter | solution.py:265
  603.8 2.0 copy.46
  605.9 43.0 %reduce-scatter.45.cloned.1.call-done = f32[256,512]{0,1:T(8,128)} async-done(((f32[1024,512]{0,1:T(8,128)}), f32[256,512]{0,1:T(8,128)}) %reduce-scatter.45.cloned.1.call-update) | async-done | bytes 524304 | tf_op jit(solution)/shard_map/reduce_scatter | solution.py:266
  650.9 43.5 %reduce-scatter.47.cloned.1.call-done = f32[128,1024]{1,0:T(8,128)} async-done(((f32[512,1024]{1,0:T(8,128)}), f32[128,1024]{1,0:T(8,128)}) %reduce-scatter.47.cloned.1.call-update) | async-done | bytes 524304 | tf_op jit(solution)/shard_map/reduce_scatter | solution.py:267
  694.4 146.8 %reduce-scatter.53.cloned.1.call-done = f32[512,1024]{1,0:T(8,128)} async-done(((f32[2048,1024]{1,0:T(8,128)}), f32[512,1024]{1,0:T(8,128)}) %reduce-scatter.53.cloned.1.call-update) | async-done | bytes 2097168 | tf_op jit(solution)/shard_map/reduce_scatter | solution.py:270
  841.2 148.0 %reduce-scatter.49.cloned.1.call-done = f32[256,2048]{1,0:T(8,128)} async-done(((f32[1024,2048]{1,0:T(8,128)}), f32[256,2048]{1,0:T(8,128)}) %reduce-scatter.49.cloned.1.call-update) | async-done | bytes 2097168 | tf_op jit(solution)/shard_map/reduce_scatter | solution.py:268
  989.2 148.2 %reduce-scatter.51.cloned.1.call-done = f32[256,2048]{1,0:T(8,128)} async-done(((f32[1024,2048]{1,0:T(8,128)}), f32[256,2048]{1,0:T(8,128)}) %reduce-scatter.51.cloned.1.call-update) | async-done | bytes 2097168 | tf_op jit(solution)/shard_map/reduce_scatter | solution.py:269
  (186 shorter events, 61.7 us)
Async XLA Ops:
  7.2 69.7 %copy-start = (bf16[512,1024]{1,0:T(8,128)(2,1)S(1)}, bf16[512,1024]{1,0:T(8,128)(2,1)}, u32[]{:S(2)}) copy-start(bf16[512,1024]{1,0:T(8,128)(2,1)} %param.27) | copy-start | bytes 3145732
  7.2 14.1 %copy-start.6 = (bf16[1024,512]{1,0:T(8,128)(2,1)S(1)}, bf16[1024,512]{1,0:T(8,128)(2,1)}, u32[]{:S(2)}) copy-start(bf16[1024,512]{1,0:T(8,128)(2,1)} %param.26) | copy-start | bytes 3145732
  7.2 27.2 %reduce-scatter.23.cloned.1.call-start = ((), (), s32[]{:S(2)}) async-start(), calls=%async_computation.20 | async-start | bytes 786432 | tf_op jit(solution)/shard_map/reduce_scatter | solution.py:166
  18.7 33.1 %reduce-scatter.21.cloned.1.call-start = ((), (), s32[]{:S(2)}) async-start(), calls=%async_computation.19 | async-start | bytes 786432 | tf_op jit(solution)/shard_map/reduce_scatter | solution.py:165
  21.3 48.7 %reduce-scatter.19.cloned.1.call-start = ((), (), s32[]{:S(2)}) async-start(), calls=%async_computation.18 | async-start | bytes 786432 | tf_op jit(solution)/shard_map/reduce_scatter | solution.py:167
  22.6 80.7 %reduce-scatter.25.cloned.1.call-start = ((), (), s32[]{:S(2)}) async-start(), calls=%async_computation.21 | async-start | bytes 1310720 | tf_op jit(solution)/shard_map/reduce_scatter | solution.py:23
  23.8 45.7 %copy-start.15 = (f32[256,64]{1,0:T(8,128)}, f32[256,64]{1,0:T(8,128)S(1)}, u32[]{:S(2)}) copy-start(f32[256,64]{1,0:T(8,128)S(1)} %get-tuple-element.112) | copy-start | bytes 196612
  24.6 44.7 %copy-start.26 = (f32[256]{0:T(256)}, f32[256]{0:T(256)S(1)}, u32[]{:S(2)}) copy-start(f32[256]{0:T(256)S(1)} %dynamic_slice.12) | copy-start | bytes 3076
  25.3 44.0 %copy-start.24 = (f32[256]{0:T(256)}, f32[256]{0:T(256)S(1)}, u32[]{:S(2)}) copy-start(f32[256]{0:T(256)S(1)} %dynamic_slice.13) | copy-start | bytes 3076
  69.5 48.0 %copy-start.16 = (bf16[256,2,64]{2,0,1:T(8,128)(2,1)}, bf16[256,2,64]{2,0,1:T(8,128)(2,1)S(1)}, u32[]{:S(2)}) copy-start(bf16[256,2,64]{2,0,1:T(8,128)(2,1)S(1)} %get-tuple-element.96) | copy-start | bytes 196612
  69.5 48.0 %copy-start.17 = (bf16[256,2,64]{2,0,1:T(8,128)(2,1)}, bf16[256,2,64]{2,0,1:T(8,128)(2,1)S(1)}, u32[]{:S(2)}) copy-start(bf16[256,2,64]{2,0,1:T(8,128)(2,1)S(1)} %get-tuple-element.97) | copy-start | bytes 196612
  69.5 48.0 %copy-start.18 = (bf16[256,2,64]{2,0,1:T(8,128)(2,1)}, bf16[256,2,64]{2,0,1:T(8,128)(2,1)S(1)}, u32[]{:S(2)}) copy-start(bf16[256,2,64]{2,0,1:T(8,128)(2,1)S(1)} %get-tuple-element.84) | copy-start | bytes 196612
  69.5 48.0 %copy-start.19 = (bf16[256,2,64]{2,0,1:T(8,128)(2,1)}, bf16[256,2,64]{2,0,1:T(8,128)(2,1)S(1)}, u32[]{:S(2)}) copy-start(bf16[256,2,64]{2,0,1:T(8,128)(2,1)S(1)} %get-tuple-element.85) | copy-start | bytes 196612
  69.5 48.0 %copy-start.20 = (bf16[256,256]{1,0:T(8,128)(2,1)S(1)}, bf16[256,256]{1,0:T(8,128)(2,1)}, u32[]{:S(2)}) copy-start(bf16[256,256]{1,0:T(8,128)(2,1)} %param.22) | copy-start | bytes 393220
  70.0 8.4 copy-start.34
  78.3 83.5 %reduce-scatter.29.cloned.1.call-start = ((), (), s32[]{:S(2)}) async-start(), calls=%async_computation.23 | async-start | bytes 3145728 | tf_op jit(solution)/shard_map/reduce_scatter | solution.py:190
  79.2 50.7 %copy-start.28 = (f32[256]{0:T(256)}, f32[256]{0:T(256)S(1)}, u32[]{:S(2)}) copy-start(f32[256]{0:T(256)S(1)} %dynamic_slice.14) | copy-start | bytes 3076
  129.8 66.6 %reduce-scatter.27.cloned.1.call-start = ((), (), s32[]{:S(2)}) async-start(), calls=%async_computation.22 | async-start | bytes 3145728 | tf_op jit(solution)/shard_map/reduce_scatter | solution.py:189
  134.7 85.9 %all-gather.4.cloned.1.call-start = ((), (), s32[]{:S(2)}) async-start(), calls=%async_computation.24 | async-start | bytes 1572864 | tf_op jit(solution)/shard_map/all_gather | solution.py:19
  199.1 64.7 %copy-start.8 = (bf16[256,256]{1,0:T(8,128)(2,1)S(1)}, bf16[256,256]{1,0:T(8,128)(2,1)}, u32[]{:S(2)}) copy-start(bf16[256,256]{1,0:T(8,128)(2,1)} %param.35) | copy-start | bytes 393220
  199.1 51.1 %reduce-scatter.31.cloned.1.call-start = ((), (), s32[]{:S(2)}) async-start(), calls=%async_computation.25 | async-start | bytes 1310720 | tf_op jit(solution)/shard_map/reduce_scatter | solution.py:23
  225.3 96.7 %reduce-scatter.33.cloned.1.call-start = ((), (), s32[]{:S(2)}) async-start(), calls=%async_computation.26 | async-start | bytes 3145728 | tf_op jit(solution)/shard_map/reduce_scatter | solution.py:27
  226.1 51.2 %copy-start.29 = (f32[256]{0:T(256)}, f32[256]{0:T(256)S(1)}, u32[]{:S(2)}) copy-start(f32[256]{0:T(256)S(1)} %dynamic_slice.15) | copy-start | bytes 3076
  290.3 56.6 %all-gather.6.cloned.1.call-start = ((), (), s32[]{:S(2)}) async-start(), calls=%async_computation.27 | async-start | bytes 1572864 | tf_op jit(solution)/shard_map/all_gather | solution.py:212
  325.5 44.9 %all-gather.8.cloned.1.call-start = ((), (), s32[]{:S(2)}) async-start(), calls=%async_computation.28 | async-start | bytes 1572864 | tf_op jit(solution)/shard_map/all_gather | solution.py:213
  326.2 74.2 %reduce-scatter.35.cloned.1.call-start = ((), (), s32[]{:S(2)}) async-start(), calls=%async_computation.29 | async-start | bytes 1310720 | tf_op jit(solution)/shard_map/reduce_scatter | solution.py:23
  351.7 48.7 %copy-start.4 = (f32[256,256]{1,0:T(8,128)S(1)}, f32[256,256]{1,0:T(8,128)}, u32[]{:S(2)}) copy-start(f32[256,256]{1,0:T(8,128)} %reduce-scatter.25.cloned.1.call-done) | copy-start | bytes 786436
  351.7 63.6 %copy-start.5 = (f32[256,256]{1,0:T(8,128)S(1)}, f32[256,256]{1,0:T(8,128)}, u32[]{:S(2)}) copy-start(f32[256,256]{1,0:T(8,128)} %reduce-scatter.31.cloned.1.call-done) | copy-start | bytes 786436
  375.5 64.3 %reduce-scatter.37.cloned.1.call-start = ((), (), s32[]{:S(2)}) async-start(), calls=%async_computation.30 | async-start | bytes 786432 | tf_op jit(solution)/shard_map/reduce_scatter | solution.py:27
  425.0 21.8 %copy-start.3 = (f32[256,256]{1,0:T(8,128)S(1)}, f32[256,256]{1,0:T(8,128)}, u32[]{:S(2)}) copy-start(f32[256,256]{1,0:T(8,128)} %reduce-scatter.21.cloned.1.call-done) | copy-start | bytes 786436
  425.0 21.8 %copy-start.27 = (f32[256]{0:T(256)S(1)}, f32[256]{0:T(256)}, u32[]{:S(2)}) copy-start(f32[256]{0:T(256)} %copy-done.26) | copy-start | bytes 3076
  425.0 130.4 %reduce-scatter.39.cloned.1.call-start = ((), (), s32[]{:S(2)}) async-start(), calls=%async_computation.31 | async-start | bytes 1310720 | tf_op jit(solution)/shard_map/reduce_scatter | solution.py:23
  440.8 7.5 copy-start.2
  440.8 7.5 copy-start.25
  440.8 7.5 copy-start.31
  445.6 25.1 %copy-start.32 = (f32[256]{0:T(256)S(1)}, f32[256]{0:T(256)}, u32[]{:S(2)}) copy-start(f32[256]{0:T(256)} %copy-done.30) | copy-start | bytes 3076
  462.3 15.0 %copy-start.23 = (bf16[2,128,256]{2,1,0:T(8,128)(2,1)S(1)}, bf16[2,128,256]{2,1,0:T(8,128)(2,1)}, u32[]{:S(2)}) copy-start(bf16[2,128,256]{2,1,0:T(8,128)(2,1)} %convolution_convert_fusion) | copy-start | bytes 393220
  462.3 22.8 %copy-start.7 = (bf16[1024,512]{1,0:T(8,128)(2,1)S(1)}, bf16[1024,512]{1,0:T(8,128)(2,1)}, u32[]{:S(2)}) copy-start(bf16[1024,512]{1,0:T(8,128)(2,1)} %param.26) | copy-start | bytes 3145732
  477.3 7.8 copy-start.10
  486.6 72.2 %reduce-scatter.41.cloned.1.call-start = ((), (), s32[]{:S(2)}) async-start(), calls=%async_computation.32 | async-start | bytes 2621440 | tf_op jit(solution)/shard_map/reduce_scatter | solution.py:264
  488.5 115.3 %reduce-scatter.43.cloned.1.call-start = ((), (), s32[]{:S(2)}) async-start(), calls=%async_computation.33 | async-start | bytes 2621440 | tf_op jit(solution)/shard_map/reduce_scatter | solution.py:265
  490.4 158.4 %reduce-scatter.45.cloned.1.call-start = ((), (), s32[]{:S(2)}) async-start(), calls=%async_computation.34 | async-start | bytes 2621440 | tf_op jit(solution)/shard_map/reduce_scatter | solution.py:266
  492.2 202.2 %reduce-scatter.47.cloned.1.call-start = ((), (), s32[]{:S(2)}) async-start(), calls=%async_computation.35 | async-start | bytes 2621440 | tf_op jit(solution)/shard_map/reduce_scatter | solution.py:267
  494.1 347.1 %reduce-scatter.53.cloned.1.call-start = ((), (), s32[]{:S(2)}) async-start(), calls=%async_computation.38 | async-start | bytes 10485760 | tf_op jit(solution)/shard_map/reduce_scatter | solution.py:270
  498.7 490.5 %reduce-scatter.49.cloned.1.call-start = ((), (), s32[]{:S(2)}) async-start(), calls=%async_computation.36 | async-start | bytes 10485760 | tf_op jit(solution)/shard_map/reduce_scatter | solution.py:268
  504.4 633.0 %reduce-scatter.51.cloned.1.call-start = ((), (), s32[]{:S(2)}) async-start(), calls=%async_computation.37 | async-start | bytes 10485760 | tf_op jit(solution)/shard_map/reduce_scatter | solution.py:269
  510.1 627.3 %copy-start.1 = (bf16[512,1024]{1,0:T(8,128)(2,1)S(1)}, bf16[512,1024]{1,0:T(8,128)(2,1)}, u32[]{:S(2)}) copy-start(bf16[512,1024]{1,0:T(8,128)(2,1)} %param.27) | copy-start | bytes 3145732
  510.1 45.3 %copy-start.9 = (f32[256,256]{1,0:T(8,128)S(1)}, f32[256,256]{1,0:T(8,128)}, u32[]{:S(2)}) copy-start(f32[256,256]{1,0:T(8,128)} %reduce-scatter.35.cloned.1.call-done) | copy-start | bytes 786436
  (12 other events, 23.8 us)
Sparse Core Ops, SparseCore 0:
  18.8 15.4 reduce-scatter.22
  37.2 14.6 reduce-scatter.20
  54.7 14.7 reduce-scatter.18
  78.5 24.8 reduce-scatter.24
  130.0 31.8 reduce-scatter.28
  164.5 31.8 reduce-scatter.26
  199.2 21.2 all-gather.3
  225.4 24.7 reduce-scatter.30
  290.4 31.5 reduce-scatter.32
  325.6 21.2 all-gather.5
  349.1 21.2 all-gather.7
  375.6 24.7 reduce-scatter.34
  425.1 14.5 reduce-scatter.36
  486.7 25.1 reduce-scatter.38
  514.1 44.6 reduce-scatter.40
  561.0 42.8 reduce-scatter.42
  606.0 42.8 reduce-scatter.44
  651.5 42.8 reduce-scatter.46
  697.3 143.7 reduce-scatter.52
  843.9 145.2 reduce-scatter.48
  992.1 145.2 reduce-scatter.50
where the time goes:
time: 1150 us; the launch traced here: 1140 us
  waiting for transfers between devices  841 us (73%)
  blocking collectives  171 us (15%)
  matrix products  69.6 us (6%)
  other arithmetic  31.6 us (3%)
  between operations  15.5 us (1%)
  local copies, waits for them, and re-layouts  14.1 us (1%)
    reduce_scatter x1, waiting for transfers between devices, body(): lax.psum_scatter(up_grad_w, 'dp', scatter_dimension=0, tiled=True)  148 us
    reduce_scatter x1, waiting for transfers between devices, body(): lax.psum_scatter(gate_grad_w, 'dp', scatter_dimension=0, tiled=True)  148 us
    reduce_scatter x1, waiting for transfers between devices, body(): lax.psum_scatter(down_grad_w, 'dp', scatter_dimension=0, tiled=True)  147 us
    reduce_scatter x4, waiting for transfers between devices, col_share(): return lax.psum_scatter(tensor, 'col', scatter_dimension=1, tiled=True)  73.2 us
    psum x4, blocking collectives, norm_total(): return lax.psum(tensor, ('row', 'col'))  50 us
    reduce_scatter x2, waiting for transfers between devices, row_back(): return lax.psum_scatter(tensor, 'row', scatter_dimension=1, tiled=True)  45.6 us
    psum x1, blocking collectives, body(): lax.psum((place_gain(query_gain_term, head_start), place_gain(key_gain_te...  43.6 us
    reduce_scatter x1, waiting for transfers between devices, body(): lax.psum_scatter(output_grad_w, 'dp', scatter_dimension=0, tiled=True)  43.5 us
  transfers between devices with their start and end apart: 21, of which 19 were waited for; matrix products, arithmetic and copies ran while one was open for 5% of the time, Pallas kernels for 0%

commit v1 on v0

v1 whole, which is shorter than its diff:
```python
import jax
import jax.numpy as jnp
from jax import lax
from jax.sharding import PartitionSpec as P

D = 2048
HD = 128

epsilon = 1e-06
rope_base = 500000.0

BF = jnp.bfloat16
F32 = jnp.float32


def mul_f32(left, right):
    return jnp.dot(left, right, preferred_element_type=F32)


def across_rows(left, right):
    return lax.dot_general(left, right, (((0,), (0,)), ((), ())), preferred_element_type=F32)


def against_cols(left, right):
    return lax.dot_general(left, right, (((1,), (1,)), ((), ())), preferred_element_type=F32)


def swap(tensor, axis, bit):
    size = lax.axis_size(axis)
    return lax.ppermute(tensor, axis, [(i, i ^ bit) for i in range(size)])


def bits_of(axis):
    size = lax.axis_size(axis)
    bits = []
    bit = 1
    while bit < size:
        bits.append(bit)
        bit *= 2
    return bits


def ordered(pieces, axis, dim):
    me = lax.axis_index(axis)
    for bit in bits_of(axis):
        flip = (me & bit) != 0
        moved = list(pieces)
        for j in range(len(pieces)):
            if not j & bit:
                moved[j] = jnp.where(flip, pieces[j | bit], pieces[j])
                moved[j | bit] = jnp.where(flip, pieces[j], pieces[j | bit])
        pieces = moved
    return jnp.concatenate(pieces, dim)


def gather_pieces(tensor, axis, dim):
    pieces = {0: tensor}
    width = tensor.shape[dim]
    for bit in reversed(bits_of(axis)):
        keys = sorted(pieces)
        packed = jnp.concatenate([pieces[k] for k in keys], dim) if len(keys) > 1 else pieces[0]
        got = swap(packed, axis, bit)
        for place, k in enumerate(keys):
            pieces[k | bit] = lax.slice_in_dim(got, place * width, (place + 1) * width, axis=dim)
    return [pieces[j] for j in range(lax.axis_size(axis))]


def gather(tensor, axis, dim=1):
    return ordered(gather_pieces(tensor, axis, dim), axis, dim)


def share(tensor, index, width):
    return lax.dynamic_slice_in_dim(tensor, index * width, width, 1)


def scatter_sum(tensor, axis, kind=BF):
    size = lax.axis_size(axis)
    me = lax.axis_index(axis)
    width = tensor.shape[1] // size
    held = {j: share(tensor, me ^ j, width) for j in range(size)}
    for bit in bits_of(axis):
        away = [j for j in sorted(held) if j & bit]
        packed = jnp.concatenate([held[j].astype(kind) for j in away], 1)
        got = swap(packed, axis, bit)
        for place, j in enumerate(away):
            part = lax.slice_in_dim(got, place * width, (place + 1) * width, axis=1)
            held[j ^ bit] = held[j ^ bit] + part.astype(F32)
            del held[j]
    return held[0]


def total(tensor):
    for axis in ("col", "row"):
        for bit in bits_of(axis):
            tensor = tensor + swap(tensor, axis, bit)
    return tensor


def dp_share(tensor):
    return lax.all_to_all(tensor, "dp", 1, 0, tiled=True)


def dp_whole(tensor):
    size = lax.axis_size("dp")
    spread = jnp.broadcast_to(tensor[None], (size,) + tensor.shape)
    got = lax.all_to_all(spread, "dp", 0, 0, tiled=True)
    return got.reshape((size * tensor.shape[0], tensor.shape[1]))


def rope_tables(row_count):
    positions = jnp.arange(row_count, dtype=F32)
    rates = rope_base ** (-2.0 * jnp.arange(HD // 2, dtype=F32) / HD)
    angles = positions[:, None] * rates[None, :]
    return (jnp.cos(angles), jnp.sin(angles))


def rotate(tensor, cosine, sine):
    half = HD // 2
    parts = []
    for start in range(0, tensor.shape[1], HD):
        first = tensor[:, start : start + half]
        second = tensor[:, start + half : start + HD]
        parts.append(first * cosine - second * sine)
        parts.append(second * cosine + first * sine)
    return jnp.concatenate(parts, 1)


def heads_of(tensor):
    return [tensor[:, s : s + HD] for s in range(0, tensor.shape[1], HD)]


def attend_forward(queries, keys, values, seq_length):
    count = queries.shape[0]
    query_pos = jnp.arange(count)[:, None]
    key_pos = jnp.arange(count)[None, :]
    allowed = (key_pos <= query_pos) & (key_pos < seq_length)
    outputs, probs = [], []
    for q, k, v in zip(heads_of(queries), heads_of(keys), heads_of(values)):
        scores = jnp.where(allowed, against_cols(q, k) * HD ** (-0.5), -1e30)
        row_max = jnp.max(scores, axis=-1, keepdims=True)
        exponent = jnp.exp(scores - row_max)
        p = exponent / jnp.sum(exponent, axis=-1, keepdims=True)
        probs.append(p)
        outputs.append(mul_f32(p.astype(BF), v))
    return jnp.concatenate(outputs, 1), probs


def attend_backward(queries, keys, values, grad_attended, probs):
    scale = HD ** (-0.5)
    gq, gk, gv = [], [], []
    for q, k, v, g, p in zip(
        heads_of(queries), heads_of(keys), heads_of(values), heads_of(grad_attended), probs
    ):
        grad_prob = against_cols(g, v)
        centre = jnp.sum(p * grad_prob, axis=-1, keepdims=True)
        grad_scores = (p * (grad_prob - centre)).astype(BF)
        gq.append(mul_f32(grad_scores, k) * scale)
        gk.append(across_rows(grad_scores, q) * scale)
        gv.append(across_rows(p.astype(BF), g))
    return jnp.concatenate(gq, 1), jnp.concatenate(gk, 1), jnp.concatenate(gv, 1)


def norm_backward(grad_norm, source, scale_rows, gain_part, stat_sum):
    weighted = grad_norm * gain_part
    return scale_rows * weighted - source * scale_rows**3 * stat_sum[:, None] / D


def place_gain(term, offset):
    return lax.dynamic_update_slice_in_dim(jnp.zeros((D,), F32), term, offset, 0)


def body(
    hidden_in,
    seq_lengths,
    query_weight,
    key_weight,
    value_weight,
    output_weight,
    gate_weight,
    up_weight,
    down_weight,
    query_gain,
    key_gain,
    mixer_gain,
    feed_gain,
    out_grad,
):
    row_count, width = hidden_in.shape
    row_place = lax.axis_index("row")
    col_place = lax.axis_index("col")
    col_size = lax.axis_size("col")
    feature_start = (row_place * col_size + col_place) * width
    block_start = row_place * col_size * width
    block_width = col_size * width
    head_start = (col_place * lax.axis_size("row") + row_place) * width
    query_gain_part = lax.dynamic_slice_in_dim(query_gain, head_start, width)
    key_gain_part = lax.dynamic_slice_in_dim(key_gain, head_start, width)
    mixer_gain_part = lax.dynamic_slice_in_dim(mixer_gain, feature_start, width)
    feed_gain_part = lax.dynamic_slice_in_dim(feed_gain, feature_start, width)
    mixer_gain_block = lax.dynamic_slice_in_dim(mixer_gain, block_start, block_width)
    feed_gain_block = lax.dynamic_slice_in_dim(feed_gain, block_start, block_width)
    seq_length = seq_lengths[0]
    cosine, sine = rope_tables(row_count)

    input_block = gather(hidden_in, "col")
    query_part = mul_f32(input_block, query_weight)
    key_part = mul_f32(input_block, key_weight)
    value_part = mul_f32(input_block, value_weight)
    query = scatter_sum(query_part, "row", F32)
    key_proj = scatter_sum(key_part, "row", F32)
    value_low = scatter_sum(value_part, "row").astype(BF)
    square_sums = total(jnp.stack([jnp.sum(query * query, 1), jnp.sum(key_proj * key_proj, 1)]))
    query_scale = lax.rsqrt(square_sums[0] / D + epsilon)[:, None]
    key_scale = lax.rsqrt(square_sums[1] / D + epsilon)[:, None]
    query_rot = rotate(query * query_scale * query_gain_part, cosine, sine).astype(BF)
    key_rot = rotate(key_proj * key_scale * key_gain_part, cosine, sine).astype(BF)
    attended, probs = attend_forward(query_rot, key_rot, value_low, seq_length)
    attended_rows = gather(attended.astype(BF), "row")
    mixer_out = scatter_sum(mul_f32(attended_rows, output_weight), "col")
    mixer_block = gather(mixer_out.astype(BF), "col").astype(F32)
    mixer_scale = lax.rsqrt(total(jnp.sum(mixer_out * mixer_out, 1)) / D + epsilon)[:, None]
    residual = hidden_in.astype(F32) + mixer_out * mixer_scale * mixer_gain_part
    residual_block = (
        input_block.astype(F32) + mixer_block * mixer_scale * mixer_gain_block
    ).astype(BF)

    gate_val = scatter_sum(mul_f32(residual_block, gate_weight), "row")
    up_val = scatter_sum(mul_f32(residual_block, up_weight), "row")
    sigmoid_val = jax.nn.sigmoid(gate_val)
    activated = gate_val * sigmoid_val
    hidden_low = (activated * up_val).astype(BF)
    hidden_rows = gather(hidden_low, "row")
    feed_out = scatter_sum(mul_f32(hidden_rows, down_weight), "col")
    feed_block = gather(feed_out.astype(BF), "col").astype(F32)

    valid = (jnp.arange(row_count) < seq_length)[:, None]
    grad_block = jnp.where(valid, gather(out_grad, "col").astype(F32), 0.0)
    grad_out = jnp.where(valid, out_grad.astype(F32), 0.0)
    feed_sums = total(
        jnp.stack(
            [jnp.sum(feed_out * feed_out, 1), jnp.sum(grad_out * feed_gain_part * feed_out, 1)]
        )
    )
    feed_scale = lax.rsqrt(feed_sums[0] / D + epsilon)[:, None]
    block_out = (residual + feed_out * feed_scale * feed_gain_part).astype(BF)
    feed_gain_term = jnp.sum(grad_out * feed_out * feed_scale, 0)
    grad_feed = norm_backward(grad_out, feed_out, feed_scale, feed_gain_part, feed_sums[1])
    grad_feed_block = norm_backward(
        grad_block, feed_block, feed_scale, feed_gain_block, feed_sums[1]
    ).astype(BF)

    grad_hidden = scatter_sum(against_cols(grad_feed_block, down_weight), "row")
    grad_gate = (
        grad_hidden * up_val * sigmoid_val * (1.0 + gate_val * (1.0 - sigmoid_val))
    ).astype(BF)
    grad_up = (grad_hidden * activated).astype(BF)
    gate_rows = gather(grad_gate, "row")
    up_rows = gather(grad_up, "row")
    grad_residual = grad_out + scatter_sum(
        against_cols(gate_rows, gate_weight) + against_cols(up_rows, up_weight), "col"
    )
    residual_grad_block = gather(grad_residual.astype(BF), "col").astype(F32)
    mixer_gain_term = jnp.sum(grad_residual * mixer_out * mixer_scale, 0)
    mixer_stat = total(jnp.sum(grad_residual * mixer_gain_part * mixer_out, 1))
    grad_mixer = norm_backward(grad_residual, mixer_out, mixer_scale, mixer_gain_part, mixer_stat)
    grad_mixer_block = norm_backward(
        residual_grad_block, mixer_block, mixer_scale, mixer_gain_block, mixer_stat
    ).astype(BF)

    grad_attended = scatter_sum(against_cols(grad_mixer_block, output_weight), "row").astype(BF)
    grad_query_rot, grad_key_rot, grad_value = attend_backward(
        query_rot, key_rot, value_low, grad_attended, probs
    )
    grad_query_norm = rotate(grad_query_rot, cosine, -sine)
    grad_key_norm = rotate(grad_key_rot, cosine, -sine)
    query_gain_term = jnp.sum(grad_query_norm * query * query_scale, 0)
    key_gain_term = jnp.sum(grad_key_norm * key_proj * key_scale, 0)
    stats = total(
        jnp.stack(
            [
                jnp.sum(grad_query_norm * query_gain_part * query, 1),
                jnp.sum(grad_key_norm * key_gain_part * key_proj, 1),
            ]
        )
    )
    grad_query = norm_backward(
        grad_query_norm, query, query_scale, query_gain_part, stats[0]
    ).astype(BF)
    grad_key = norm_backward(
        grad_key_norm, key_proj, key_scale, key_gain_part, stats[1]
    ).astype(BF)
    grad_value_low = grad_value.astype(BF)
    query_rows = gather(grad_query, "row")
    key_rows = gather(grad_key, "row")
    value_rows = gather(grad_value_low, "row")
    grad_input = grad_residual + scatter_sum(
        against_cols(query_rows, query_weight)
        + against_cols(key_rows, key_weight)
        + against_cols(value_rows, value_weight),
        "col",
    )

    input_all = dp_share(input_block)
    residual_all = dp_share(residual_block)
    attended_all = dp_share(attended_rows)
    hidden_all = dp_share(hidden_rows)
    feed_all = gather(dp_whole(grad_feed.astype(BF)), "col")
    gate_all = gather(dp_whole(grad_gate), "row")
    up_all = gather(dp_whole(grad_up), "row")
    mixer_all = gather(dp_whole(grad_mixer.astype(BF)), "col")
    query_all = gather(dp_whole(grad_query), "row")
    key_all = gather(dp_whole(grad_key), "row")
    value_all = gather(dp_whole(grad_value_low), "row")
    gain_sums = lax.psum(
        (
            place_gain(query_gain_term, head_start),
            place_gain(key_gain_term, head_start),
            place_gain(mixer_gain_term, feature_start),
            place_gain(feed_gain_term, feature_start),
        ),
        ("dp", "row", "col"),
    )
    return (
        block_out,
        grad_input.astype(BF),
        across_rows(input_all, query_all),
        across_rows(input_all, key_all),
        across_rows(input_all, value_all),
        across_rows(attended_all, mixer_all),
        across_rows(residual_all, gate_all),
        across_rows(residual_all, up_all),
        across_rows(hidden_all, feed_all),
        *gain_sums,
    )


def solution(mesh):
    in_specs = (
        P("dp", ("row", "col")),
        P("dp"),
        P("row", "col"),
        P("row", "col"),
        P("row", "col"),
        P("col", "row"),
        P("row", "col"),
        P("row", "col"),
        P("col", "row"),
        P(),
        P(),
        P(),
        P(),
        P("dp", ("row", "col")),
    )
    out_specs = (
        P("dp", ("row", "col")),
        P("dp", ("row", "col")),
        P(("row", "dp"), "col"),
        P(("row", "dp"), "col"),
        P(("row", "dp"), "col"),
        P(("col", "dp"), "row"),
        P(("row", "dp"), "col"),
        P(("row", "dp"), "col"),
        P(("col", "dp"), "row"),
        P(),
        P(),
        P(),
        P(),
    )
    return jax.shard_map(body, mesh=mesh, in_specs=in_specs, out_specs=out_specs, check_vma=False)
```

time: 1150 us -> 556 us (0.48)
  waiting for transfers between devices: 841 us -> 211 us
  starting transfers between devices: 1.27 us -> 98.3 us
  blocking collectives: 171 us -> 126 us
  matrix products: 69.6 us -> 46.3 us
  other arithmetic: 31.6 us -> 50.9 us
  between operations: 15.5 us -> 3.28 us
    reduce_scatter x18 -> x0, waiting for transfers between devices: 779 us -> none  [the longest x1 148 us: body(): lax.psum_scatter(up_grad_w, 'dp', scatter_dimension=0, tiled=True)]
    ppermute x0 -> x56, waiting for transfers between devices: none -> 180 us  [swap(): return lax.ppermute(tensor, axis, [(i, i ^ bit) for i in range(size)])]
    psum x6 -> x0, blocking collectives: 75.9 us -> none  [the longest x4 50 us: norm_total(): return lax.psum(tensor, ('row', 'col'))]
    all_to_all x0 -> x2, blocking collectives: none -> 66 us  [dp_whole(): got = lax.all_to_all(spread, 'dp', 0, 0, tiled=True)]
    ppermute x0 -> x56, starting transfers between devices: none -> 60.7 us  [swap(): return lax.ppermute(tensor, axis, [(i, i ^ bit) for i in range(size)])]
    all_gather x3 -> x0, waiting for transfers between devices: 60.5 us -> none  [the longest x1 21.4 us: row_whole(): return lax.all_gather(tensor, 'row', axis=1, tiled=True)]
    all_gather x8 -> x0, blocking collectives: 51.8 us -> none  [the longest x4 28.8 us: widen(): return lax.all_gather(tensor, 'col', axis=1, tiled=True)]
    all_to_all x0 -> x9, starting transfers between devices: none -> 37.7 us  [the longest x5 20.6 us: dp_whole(): got = lax.all_to_all(spread, 'dp', 0, 0, tiled=True)]
  transfers between devices with their start and end apart: 21 -> 65, of which waited for: 19 -> 46; matrix products, arithmetic and copies ran while one was open for 5% -> 15% of each run, Pallas kernels for 0% -> 0%
where the time goes in v1:
time: 556 us; the launch traced here: 554 us
  waiting for transfers between devices  211 us (38%)
  blocking collectives  126 us (23%)
  starting transfers between devices  98.3 us (18%)
  other arithmetic  50.9 us (9%)
  matrix products  46.3 us (8%)
  local copies, waits for them, and re-layouts  18.5 us (3%)
    ppermute x56, waiting for transfers between devices, swap(): return lax.ppermute(tensor, axis, [(i, i ^ bit) for i in range(size)])  180 us
    all_to_all x2, blocking collectives, dp_whole(): got = lax.all_to_all(spread, 'dp', 0, 0, tiled=True)  66 us
    ppermute x56, starting transfers between devices, swap(): return lax.ppermute(tensor, axis, [(i, i ^ bit) for i in range(size)])  60.7 us
    psum x1, blocking collectives, body(): lax.psum((place_gain(query_gain_term, head_start), place_gain(key_gain_te...  59.9 us
    all_to_all x5, waiting for transfers between devices, dp_whole(): got = lax.all_to_all(spread, 'dp', 0, 0, tiled=True)  26.4 us
    dot_general x11, matrix products, across_rows(): lax.dot_general(left, right, (((0,), (0,)), ((), ())), preferred_element_...  22.5 us
    all_to_all x5, starting transfers between devices, dp_whole(): got = lax.all_to_all(spread, 'dp', 0, 0, tiled=True)  20.6 us
    select_n x19, other arithmetic, ordered(): moved[j] = jnp.where(flip, pieces[j | bit], pieces[j])  20.5 us
  transfers between devices with their start and end apart: 65, of which 46 were waited for; matrix products, arithmetic and copies ran while one was open for 15% of the time, Pallas kernels for 0%

profile of v1, /device:TPU:0, one launch (start us, length us, event | category | flops | bytes accessed | tf_op | source)
XLA Modules:
  0.0 554.3 jit_solution(2481437988915258687)
XLA Ops:
  0.7 3.0 collective-permute-start
  3.7 3.7 collective-permute-done
  18.2 4.9 collective-permute-done.3
  24.2 3.8 collective-permute-done.2
  42.8 3.2 collective-permute-done.8
  51.6 3.9 collective-permute-done.10
  58.3 3.3 collective-permute-done.14
  71.0 3.7 fusion.164
  76.7 2.4 fusion.166
  79.8 9.9 %collective-permute-done.17 = bf16[256,1024]{1,0:T(8,128)(2,1)S(1)} collective-permute-done((bf16[256,1024]{1,0:T(8,128)(2,1)S(1)}, bf16[256,1024]{1,0:T(8,128)(2,1)S(1)}, u32[]{:S(2)}, u32[]{:S(2)}) %collective-permute-start.17) | collective-permute-done | bytes 524320 | tf_op jit(solution)/shard_map/ppermute | solution.py:30
  89.7 8.3 %collective-permute-done.16 = bf16[256,1024]{1,0:T(8,128)(2,1)S(1)} collective-permute-done((bf16[256,1024]{1,0:T(8,128)(2,1)S(1)}, bf16[256,1024]{1,0:T(8,128)(2,1)S(1)}, u32[]{:S(2)}, u32[]{:S(2)}) %collective-permute-start.16) | collective-permute-done | bytes 524320 | tf_op jit(solution)/shard_map/ppermute | solution.py:30
  100.3 9.2 %collective-permute-done.18 = bf16[256,1024]{1,0:T(8,128)(2,1)S(1)} collective-permute-done((bf16[256,1024]{1,0:T(8,128)(2,1)S(1)}, bf16[256,1024]{1,0:T(8,128)(2,1)S(1)}, u32[]{:S(2)}, u32[]{:S(2)}) %collective-permute-start.18) | collective-permute-done | bytes 524320 | tf_op jit(solution)/shard_map/ppermute | solution.py:30
  116.1 3.7 collective-permute-done.20
  135.7 12.2 %collective-permute-done.28 = bf16[256,1024]{1,0:T(8,128)(2,1)S(1)} collective-permute-done((bf16[256,1024]{1,0:T(8,128)(2,1)S(1)}, bf16[256,1024]{1,0:T(8,128)(2,1)S(1)}, u32[]{:S(2)}, u32[]{:S(2)}) %collective-permute-start.28) | collective-permute-done | bytes 524320 | tf_op jit(solution)/shard_map/ppermute | solution.py:30
  150.8 12.8 %collective-permute-done.30 = bf16[256,1024]{1,0:T(8,128)(2,1)S(1)} collective-permute-done((bf16[256,1024]{1,0:T(8,128)(2,1)S(1)}, bf16[256,1024]{1,0:T(8,128)(2,1)S(1)}, u32[]{:S(2)}, u32[]{:S(2)}) %collective-permute-start.30) | collective-permute-done | bytes 524320 | tf_op jit(solution)/shard_map/ppermute | solution.py:30
  164.9 8.2 %collective-permute-done.29 = bf16[256,1024]{1,0:T(8,128)(2,1)S(1)} collective-permute-done((bf16[256,1024]{1,0:T(8,128)(2,1)S(1)}, bf16[256,1024]{1,0:T(8,128)(2,1)S(1)}, u32[]{:S(2)}, u32[]{:S(2)}) %collective-permute-start.29) | collective-permute-done | bytes 524320 | tf_op jit(solution)/shard_map/ppermute | solution.py:30
  178.8 3.0 collective-permute-done.32
  190.9 5.1 all-to-all-start
  205.2 2.9 collective-permute-done.38
  221.7 5.1 all-to-all-start.10
  232.6 6.6 %all-to-all-done.10 = bf16[4,256,256]{2,1,0:T(8,128)(2,1)S(1)} async-done(((bf16[4,256,256]{2,1,0:T(8,128)(2,1)}), bf16[4,256,256]{2,1,0:T(8,128)(2,1)S(1)}, u32[]{:S(2)}, u32[]{:S(2)}) %all-to-all-start.10) | async-done | bytes 524320 | tf_op jit(solution)/shard_map/all_to_all | solution.py:106
  240.1 3.5 all-to-all-start.3
  247.9 8.0 %all-to-all-done.3 = bf16[4,256,256]{2,1,0:T(8,128)(2,1)S(1)} async-done(((bf16[4,256,256]{2,1,0:T(8,128)(2,1)}), bf16[4,256,256]{2,1,0:T(8,128)(2,1)S(1)}, u32[]{:S(2)}, u32[]{:S(2)}) %all-to-all-start.3) | async-done | bytes 524320 | tf_op jit(solution)/shard_map/all_to_all | solution.py:106
  257.7 4.1 all-to-all-start.1
  266.7 6.9 %all-to-all-done.1 = bf16[4,256,256]{2,1,0:T(8,128)(2,1)} async-done(((bf16[4,256,256]{2,1,0:T(8,128)(2,1)}), bf16[4,256,256]{2,1,0:T(8,128)(2,1)}, u32[]{:S(2)}, u32[]{:S(2)}) %all-to-all-start.1) | async-done | bytes 524320 | tf_op jit(solution)/shard_map/all_to_all | solution.py:106
  274.4 4.1 all-to-all-start.2
  280.2 3.5 collective-permute-done.46
  285.4 4.9 all-to-all-done.2
  290.3 15.6 %all_to_all.108 = bf16[4,256,256]{2,1,0:T(8,128)(2,1)S(1)} all-to-all(bf16[4,256,256]{2,1,0:T(8,128)(2,1)S(1)} %broadcast_in_dim.51), channel_id=1, replica_groups=mesh['dp'=4,'row'=2,'col'=4] {'dp'}, dimensions={0} | all-to-all | bytes 1048576 | tf_op jit(solution)/shard_map/all_to_all | solution.py:106
  306.2 50.4 %all_to_all.109 = bf16[4,256,1024]{2,1,0:T(8,128)(2,1)} all-to-all(bf16[4,256,1024]{2,1,0:T(8,128)(2,1)S(1)} %broadcast_in_dim.52), channel_id=1, replica_groups=mesh['dp'=4,'row'=2,'col'=4] {'dp'}, dimensions={0} | all-to-all | bytes 4194304 | tf_op jit(solution)/shard_map/all_to_all | solution.py:106
  358.1 3.7 all-to-all-start.8
  365.8 2.3 add_convert_fusion
  370.4 59.9 %all-reduce = (f32[2048]{0:T(1024)}, f32[2048]{0:T(1024)}, f32[2048]{0:T(1024)}, f32[2048]{0:T(1024)}) all-reduce(f32[2048]{0:T(1024)S(1)} %dynamic_update_slice.12, f32[2048]{0:T(1024)S(1)} %dynamic_update_slice.13, f32[2048]{0:T(1024)S(1)} %dynamic_update_slice.14, ...), channel_id=1, replica_groups=mesh['dp'=4,'row'=2,'col'=4] {'dp','row','col'}, use_global_device_ids=true, to_apply=%region_15.16 | all-reduce | flops 8192 | bytes 65536 | tf_op jit(solution)/shard_map/psum | solution.py:314
  436.8 4.3 all-to-all-start.9
  441.1 2.6 fusion.49
  451.2 7.9 %collective-permute-done.48 = bf16[1024,256]{1,0:T(8,128)(2,1)} collective-permute-done((bf16[1024,256]{1,0:T(8,128)(2,1)}, bf16[1024,256]{1,0:T(8,128)(2,1)}, u32[]{:S(2)}, u32[]{:S(2)}) %collective-permute-start.48) | collective-permute-done | bytes 524320 | tf_op jit(solution)/shard_map/ppermute | solution.py:30
  461.5 2.3 fusion.41
  463.8 2.3 fusion.45
  468.1 3.0 broadcast_select_fusion.15
  471.1 3.6 all-to-all-start.4
  474.7 4.5 fusion.16
  479.1 4.9 all-to-all-done.4
  484.0 4.1 all-to-all-start.6
  490.8 13.1 %collective-permute-done.52 = bf16[1024,1024]{1,0:T(8,128)(2,1)} collective-permute-done((bf16[1024,1024]{1,0:T(8,128)(2,1)}, bf16[1024,1024]{1,0:T(8,128)(2,1)}, u32[]{:S(2)}, u32[]{:S(2)}) %collective-permute-start.52) | collective-permute-done | bytes 2097184 | tf_op jit(solution)/shard_map/ppermute | solution.py:30
  504.0 4.5 broadcast_select_fusion.3
  508.5 5.0 fusion
  513.5 35.3 %collective-permute-done.53 = bf16[1024,1024]{1,0:T(8,128)(2,1)} collective-permute-done((bf16[1024,1024]{1,0:T(8,128)(2,1)S(1)}, bf16[1024,1024]{1,0:T(8,128)(2,1)}, u32[]{:S(2)}, u32[]{:S(2)}) %collective-permute-start.53) | collective-permute-done | bytes 2097184 | tf_op jit(solution)/shard_map/ppermute | solution.py:30
  550.6 3.7 fusion.4
  (464 shorter events, 164.3 us)
Async XLA Ops:
  0.7 6.7 %collective-permute-start = (bf16[256,256]{1,0:T(8,128)(2,1)}, bf16[256,256]{1,0:T(8,128)(2,1)S(1)}, u32[]{:S(2)}, u32[]{:S(2)}) collective-permute-start(bf16[256,256]{1,0:T(8,128)(2,1)} %param.14), channel_id=1, source_target_pairs={{0,2},{1,3},{2,0},{3,1},{4,6},{5,7},{6,4},{7,5},{8,10},{9,11},{10,... | collective-permute-start | bytes 393224 | tf_op jit(solution)/shard_map/ppermute | solution.py:30
  13.6 9.5 %collective-permute-start.3 = (f32[256,256]{1,0:T(8,128)}, f32[256,256]{1,0:T(8,128)}, u32[]{:S(2)}, u32[]{:S(2)}) collective-permute-start(f32[256,256]{1,0:T(8,128)} %constant_dynamic-slice_fusion), channel_id=1, source_target_pairs={{0,4},{4,0},{1,5},{5,1},{2,6},{6,2},{3,7},{7,3},{8,12},{12,8},{9,1... | collective-permute-start | bytes 786440 | tf_op jit(solution)/shard_map/ppermute | solution.py:30
  15.8 12.1 %collective-permute-start.2 = (f32[256,256]{1,0:T(8,128)S(1)}, f32[256,256]{1,0:T(8,128)}, u32[]{:S(2)}, u32[]{:S(2)}) collective-permute-start(f32[256,256]{1,0:T(8,128)S(1)} %constant_dynamic-slice_fusion.1), channel_id=1, source_target_pairs={{0,4},{4,0},{1,5},{5,1},{2,6},{6,2},{3,7},{7,3},{8,12},{12,8},{9,1... | collective-permute-start | bytes 786440 | tf_op jit(solution)/shard_map/ppermute | solution.py:30
  32.2 5.3 collective-permute-start.7
  41.0 5.0 collective-permute-start.8
  49.8 5.7 %collective-permute-start.10 = (bf16[256,256]{1,0:T(8,128)(2,1)S(1)}, bf16[256,256]{1,0:T(8,128)(2,1)}, u32[]{:S(2)}, u32[]{:S(2)}) collective-permute-start(bf16[256,256]{1,0:T(8,128)(2,1)S(1)} %add_convert_fusion.7), channel_id=1, source_target_pairs={{0,2},{1,3},{2,0},{3,1},{4,6},{5,7},{6,4},{7,5},{8,10},{9,11},{10,... | collective-permute-start | bytes 393224 | tf_op jit(solution)/shard_map/ppermute | solution.py:30
  56.5 5.0 collective-permute-start.14
  61.6 9.3 %collective-permute-start.15 = (bf16[256,512]{1,0:T(8,128)(2,1)S(1)}, bf16[256,512]{1,0:T(8,128)(2,1)S(1)}, u32[]{:S(2)}, u32[]{:S(2)}) collective-permute-start(bf16[256,512]{1,0:T(8,128)(2,1)S(1)} %pad_maximum_fusion.8), channel_id=1, source_target_pairs={{0,1},{1,0},{2,3},{3,2},{4,5},{5,4},{6,7},{7,6},{8,9},{9,8},{10,11... | collective-permute-start | bytes 786440 | tf_op jit(solution)/shard_map/ppermute | solution.py:30
  74.9 14.9 %collective-permute-start.17 = (bf16[256,1024]{1,0:T(8,128)(2,1)S(1)}, bf16[256,1024]{1,0:T(8,128)(2,1)S(1)}, u32[]{:S(2)}, u32[]{:S(2)}) collective-permute-start(bf16[256,1024]{1,0:T(8,128)(2,1)S(1)} %dynamic-slice_convert_fusion.1), channel_id=1, source_target_pairs={{0,4},{4,0},{1,5},{5,1},{2,6},{6,2},{3,7},{7,3},{8,12},{12,8},{9,1... | collective-permute-start | bytes 1572872 | tf_op jit(solution)/shard_map/ppermute | solution.py:30
  79.3 18.8 %collective-permute-start.16 = (bf16[256,1024]{1,0:T(8,128)(2,1)S(1)}, bf16[256,1024]{1,0:T(8,128)(2,1)S(1)}, u32[]{:S(2)}, u32[]{:S(2)}) collective-permute-start(bf16[256,1024]{1,0:T(8,128)(2,1)S(1)} %dynamic-slice_convert_fusion.2), channel_id=1, source_target_pairs={{0,4},{4,0},{1,5},{5,1},{2,6},{6,2},{3,7},{7,3},{8,12},{12,8},{9,1... | collective-permute-start | bytes 1572872 | tf_op jit(solution)/shard_map/ppermute | solution.py:30
  98.5 11.1 %collective-permute-start.18 = (bf16[256,1024]{1,0:T(8,128)(2,1)S(1)}, bf16[256,1024]{1,0:T(8,128)(2,1)S(1)}, u32[]{:S(2)}, u32[]{:S(2)}) collective-permute-start(bf16[256,1024]{1,0:T(8,128)(2,1)S(1)} %multiply_convert_fusion.2), channel_id=1, source_target_pairs={{0,4},{4,0},{1,5},{5,1},{2,6},{6,2},{3,7},{7,3},{8,12},{12,8},{9,1... | collective-permute-start | bytes 1572872 | tf_op jit(solution)/shard_map/ppermute | solution.py:30
  113.3 6.5 %collective-permute-start.20 = (bf16[256,256]{1,0:T(8,128)(2,1)S(1)}, bf16[256,256]{1,0:T(8,128)(2,1)}, u32[]{:S(2)}, u32[]{:S(2)}) collective-permute-start(bf16[256,256]{1,0:T(8,128)(2,1)S(1)} %add_convert_fusion.6), channel_id=1, source_target_pairs={{0,2},{1,3},{2,0},{3,1},{4,6},{5,7},{6,4},{7,5},{8,10},{9,11},{10,... | collective-permute-start | bytes 393224 | tf_op jit(solution)/shard_map/ppermute | solution.py:30
  115.1 6.7 %collective-permute-start.24 = (bf16[256,256]{1,0:T(8,128)(2,1)S(1)}, bf16[256,256]{1,0:T(8,128)(2,1)S(1)}, u32[]{:S(2)}, u32[]{:S(2)}) collective-permute-start(bf16[256,256]{1,0:T(8,128)(2,1)S(1)} %copy-done.12), channel_id=1, source_target_pairs={{0,2},{1,3},{2,0},{3,1},{4,6},{5,7},{6,4},{7,5},{8,10},{9,11},{10,... | collective-permute-start | bytes 393224 | tf_op jit(solution)/shard_map/ppermute | solution.py:30
  121.8 6.6 %collective-permute-start.25 = (bf16[256,512]{1,0:T(8,128)(2,1)S(1)}, bf16[256,512]{1,0:T(8,128)(2,1)S(1)}, u32[]{:S(2)}, u32[]{:S(2)}) collective-permute-start(bf16[256,512]{1,0:T(8,128)(2,1)S(1)} %pad_maximum_fusion.10), channel_id=1, source_target_pairs={{0,1},{1,0},{2,3},{3,2},{4,5},{5,4},{6,7},{7,6},{8,9},{9,8},{10,11... | collective-permute-start | bytes 786440 | tf_op jit(solution)/shard_map/ppermute | solution.py:30
  124.7 5.5 collective-permute-start.26
  126.6 3.7 collective-permute-start.23
  133.9 14.0 %collective-permute-start.28 = (bf16[256,1024]{1,0:T(8,128)(2,1)S(1)}, bf16[256,1024]{1,0:T(8,128)(2,1)S(1)}, u32[]{:S(2)}, u32[]{:S(2)}) collective-permute-start(bf16[256,1024]{1,0:T(8,128)(2,1)S(1)} %dynamic-slice_convert_fusion), channel_id=1, source_target_pairs={{0,4},{4,0},{1,5},{5,1},{2,6},{6,2},{3,7},{7,3},{8,12},{12,8},{9,1... | collective-permute-start | bytes 1572872 | tf_op jit(solution)/shard_map/ppermute | solution.py:30
  148.7 14.9 %collective-permute-start.30 = (bf16[256,1024]{1,0:T(8,128)(2,1)S(1)}, bf16[256,1024]{1,0:T(8,128)(2,1)S(1)}, u32[]{:S(2)}, u32[]{:S(2)}) collective-permute-start(bf16[256,1024]{1,0:T(8,128)(2,1)S(1)} %get-tuple-element.37), channel_id=1, source_target_pairs={{0,4},{4,0},{1,5},{5,1},{2,6},{6,2},{3,7},{7,3},{8,12},{12,8},{9,1... | collective-permute-start | bytes 1572872 | tf_op jit(solution)/shard_map/ppermute | solution.py:30
  150.5 22.6 %collective-permute-start.29 = (bf16[256,1024]{1,0:T(8,128)(2,1)S(1)}, bf16[256,1024]{1,0:T(8,128)(2,1)S(1)}, u32[]{:S(2)}, u32[]{:S(2)}) collective-permute-start(bf16[256,1024]{1,0:T(8,128)(2,1)S(1)} %get-tuple-element.36), channel_id=1, source_target_pairs={{0,4},{4,0},{1,5},{5,1},{2,6},{6,2},{3,7},{7,3},{8,12},{12,8},{9,1... | collective-permute-start | bytes 1572872 | tf_op jit(solution)/shard_map/ppermute | solution.py:30
  176.3 5.6 %collective-permute-start.32 = (bf16[256,256]{1,0:T(8,128)(2,1)S(1)}, bf16[256,256]{1,0:T(8,128)(2,1)S(1)}, u32[]{:S(2)}, u32[]{:S(2)}) collective-permute-start(bf16[256,256]{1,0:T(8,128)(2,1)S(1)} %add_convert_fusion.4), channel_id=1, source_target_pairs={{0,2},{1,3},{2,0},{3,1},{4,6},{5,7},{6,4},{7,5},{8,10},{9,11},{10,... | collective-permute-start | bytes 393224 | tf_op jit(solution)/shard_map/ppermute | solution.py:30
  183.5 5.0 collective-permute-start.33
  187.0 8.9 %collective-permute-start.36 = (f32[256]{0:T(256)}, f32[256]{0:T(256)}, u32[]{:S(2)}, u32[]{:S(2)}) collective-permute-start(f32[256]{0:T(256)} %add.320), channel_id=1, source_target_pairs={{0,2},{1,3},{2,0},{3,1},{4,6},{5,7},{6,4},{7,5},{8,10},{9,11},{10,... | collective-permute-start | bytes 3080 | tf_op jit(solution)/shard_map/ppermute | solution.py:30
  189.9 10.3 %collective-permute-start.34 = (bf16[256,512]{1,0:T(8,128)(2,1)}, bf16[256,512]{1,0:T(8,128)(2,1)}, u32[]{:S(2)}, u32[]{:S(2)}) collective-permute-start(bf16[256,512]{1,0:T(8,128)(2,1)} %pad_maximum_fusion.13), channel_id=1, source_target_pairs={{0,1},{1,0},{2,3},{3,2},{4,5},{5,4},{6,7},{7,6},{8,9},{9,8},{10,11... | collective-permute-start | bytes 786440 | tf_op jit(solution)/shard_map/ppermute | solution.py:30
  190.9 30.0 %all-to-all-start = ((bf16[256,4,256]{2,0,1:T(8,128)(2,1)}), bf16[256,4,256]{2,0,1:T(8,128)(2,1)}, u32[]{:S(2)}, u32[]{:S(2)}) async-start(bf16[256,4,256]{2,0,1:T(8,128)(2,1)} %bitcast.105), calls=%async_computation | async-start | bytes 1048576 | tf_op jit(solution)/shard_map/all_to_all | solution.py:100
  203.1 5.0 collective-permute-start.38
  217.2 3.7 collective-permute-start.41
  218.8 13.1 %collective-permute-start.44 = (bf16[256,256]{1,0:T(8,128)(2,1)S(1)}, bf16[256,256]{1,0:T(8,128)(2,1)S(1)}, u32[]{:S(2)}, u32[]{:S(2)}) collective-permute-start(bf16[256,256]{1,0:T(8,128)(2,1)S(1)} %pad_maximum_fusion.19), channel_id=1, source_target_pairs={{0,4},{4,0},{1,5},{5,1},{2,6},{6,2},{3,7},{7,3},{8,12},{12,8},{9,1... | collective-permute-start | bytes 393224 | tf_op jit(solution)/shard_map/ppermute | solution.py:30
  221.7 17.6 %all-to-all-start.10 = ((bf16[4,256,256]{2,1,0:T(8,128)(2,1)}), bf16[4,256,256]{2,1,0:T(8,128)(2,1)S(1)}, u32[]{:S(2)}, u32[]{:S(2)}) async-start(bf16[4,256,256]{2,1,0:T(8,128)(2,1)} %broadcast_in_dim.54), calls=%async_computation.10 | async-start | bytes 1048576 | tf_op jit(solution)/shard_map/all_to_all | solution.py:106
  228.2 17.3 %collective-permute-start.43 = (bf16[256,256]{1,0:T(8,128)(2,1)S(1)}, bf16[256,256]{1,0:T(8,128)(2,1)}, u32[]{:S(2)}, u32[]{:S(2)}) collective-permute-start(bf16[256,256]{1,0:T(8,128)(2,1)S(1)} %subtract_convert_fusion.4), channel_id=1, source_target_pairs={{0,4},{4,0},{1,5},{5,1},{2,6},{6,2},{3,7},{7,3},{8,12},{12,8},{9,1... | collective-permute-start | bytes 393224 | tf_op jit(solution)/shard_map/ppermute | solution.py:30
  231.4 30.5 %collective-permute-start.42 = (bf16[256,256]{1,0:T(8,128)(2,1)}, bf16[256,256]{1,0:T(8,128)(2,1)}, u32[]{:S(2)}, u32[]{:S(2)}) collective-permute-start(bf16[256,256]{1,0:T(8,128)(2,1)} %subtract_convert_fusion.5), channel_id=1, source_target_pairs={{0,4},{4,0},{1,5},{5,1},{2,6},{6,2},{3,7},{7,3},{8,12},{12,8},{9,1... | collective-permute-start | bytes 393224 | tf_op jit(solution)/shard_map/ppermute | solution.py:30
  240.1 15.8 %all-to-all-start.3 = ((bf16[4,256,256]{2,1,0:T(8,128)(2,1)}), bf16[4,256,256]{2,1,0:T(8,128)(2,1)S(1)}, u32[]{:S(2)}, u32[]{:S(2)}) async-start(bf16[4,256,256]{2,1,0:T(8,128)(2,1)} %broadcast_in_dim.50), calls=%async_computation.3 | async-start | bytes 1048576 | tf_op jit(solution)/shard_map/all_to_all | solution.py:106
  257.7 15.9 %all-to-all-start.1 = ((bf16[4,256,256]{2,1,0:T(8,128)(2,1)}), bf16[4,256,256]{2,1,0:T(8,128)(2,1)}, u32[]{:S(2)}, u32[]{:S(2)}) async-start(bf16[4,256,256]{2,1,0:T(8,128)(2,1)} %broadcast_in_dim.48), calls=%async_computation.1 | async-start | bytes 1048576 | tf_op jit(solution)/shard_map/all_to_all | solution.py:106
  266.7 11.9 %collective-permute-start.45 = (bf16[256,512]{1,0:T(8,128)(2,1)}, bf16[256,512]{1,0:T(8,128)(2,1)S(1)}, u32[]{:S(2)}, u32[]{:S(2)}) collective-permute-start(bf16[256,512]{1,0:T(8,128)(2,1)} %pad_maximum_fusion.16), channel_id=1, source_target_pairs={{0,1},{1,0},{2,3},{3,2},{4,5},{5,4},{6,7},{7,6},{8,9},{9,8},{10,11... | collective-permute-start | bytes 786440 | tf_op jit(solution)/shard_map/ppermute | solution.py:30
  274.4 15.9 %all-to-all-start.2 = ((bf16[4,256,256]{2,1,0:T(8,128)(2,1)}), bf16[4,256,256]{2,1,0:T(8,128)(2,1)}, u32[]{:S(2)}, u32[]{:S(2)}) async-start(bf16[4,256,256]{2,1,0:T(8,128)(2,1)} %broadcast_in_dim.49), calls=%async_computation.2 | async-start | bytes 1048576 | tf_op jit(solution)/shard_map/all_to_all | solution.py:106
  278.6 5.0 collective-permute-start.46
  358.1 78.7 %all-to-all-start.8 = ((bf16[4,256,1024]{2,1,0:T(8,128)(2,1)}), bf16[4,256,1024]{2,1,0:T(8,128)(2,1)S(1)}, u32[]{:S(2)}, u32[]{:S(2)}) async-start(bf16[4,256,1024]{2,1,0:T(8,128)(2,1)} %broadcast_in_dim.53), calls=%async_computation.8 | async-start | bytes 4194304 | tf_op jit(solution)/shard_map/all_to_all | solution.py:106
  361.9 68.3 %collective-permute-start.54 = (bf16[1024,256]{1,0:T(8,128)(2,1)S(1)}, bf16[1024,256]{1,0:T(8,128)(2,1)}, u32[]{:S(2)}, u32[]{:S(2)}) collective-permute-start(bf16[1024,256]{1,0:T(8,128)(2,1)S(1)} %bitcast.98), channel_id=1, source_target_pairs={{0,2},{1,3},{2,0},{3,1},{4,6},{5,7},{6,4},{7,5},{8,10},{9,11},{10,... | collective-permute-start | bytes 1572872 | tf_op jit(solution)/shard_map/ppermute | solution.py:30
  364.3 70.5 %collective-permute-start.49 = (bf16[1024,256]{1,0:T(8,128)(2,1)}, bf16[1024,256]{1,0:T(8,128)(2,1)}, u32[]{:S(2)}, u32[]{:S(2)}) collective-permute-start(bf16[1024,256]{1,0:T(8,128)(2,1)} %bitcast.104), channel_id=1, source_target_pairs={{0,4},{4,0},{1,5},{5,1},{2,6},{6,2},{3,7},{7,3},{8,12},{12,8},{9,1... | collective-permute-start | bytes 1572872 | tf_op jit(solution)/shard_map/ppermute | solution.py:30
  432.4 35.7 %collective-permute-start.55 = (bf16[1024,512]{1,0:T(8,128)(2,1)}, bf16[1024,512]{1,0:T(8,128)(2,1)}, u32[]{:S(2)}, u32[]{:S(2)}) collective-permute-start(bf16[1024,512]{1,0:T(8,128)(2,1)} %pad_maximum_fusion.2), channel_id=1, source_target_pairs={{0,1},{1,0},{2,3},{3,2},{4,5},{5,4},{6,7},{7,6},{8,9},{9,8},{10,11... | collective-permute-start | bytes 3145736 | tf_op jit(solution)/shard_map/ppermute | solution.py:30
  432.4 15.4 %collective-permute-start.47 = (bf16[1024,256]{1,0:T(8,128)(2,1)}, bf16[1024,256]{1,0:T(8,128)(2,1)}, u32[]{:S(2)}, u32[]{:S(2)}) collective-permute-start(bf16[1024,256]{1,0:T(8,128)(2,1)} %bitcast.15), channel_id=1, source_target_pairs={{0,4},{4,0},{1,5},{5,1},{2,6},{6,2},{3,7},{7,3},{8,12},{12,8},{9,1... | collective-permute-start | bytes 1572872 | tf_op jit(solution)/shard_map/ppermute | solution.py:30
  434.7 24.3 %collective-permute-start.48 = (bf16[1024,256]{1,0:T(8,128)(2,1)}, bf16[1024,256]{1,0:T(8,128)(2,1)}, u32[]{:S(2)}, u32[]{:S(2)}) collective-permute-start(bf16[1024,256]{1,0:T(8,128)(2,1)} %bitcast.17), channel_id=1, source_target_pairs={{0,4},{4,0},{1,5},{5,1},{2,6},{6,2},{3,7},{7,3},{8,12},{12,8},{9,1... | collective-permute-start | bytes 1572872 | tf_op jit(solution)/shard_map/ppermute | solution.py:30
  436.8 34.3 %all-to-all-start.9 = ((bf16[256,4,512]{2,0,1:T(8,128)(2,1)}), bf16[256,4,512]{2,0,1:T(8,128)(2,1)}, u32[]{:S(2)}, u32[]{:S(2)}) async-start(bf16[256,4,512]{2,0,1:T(8,128)(2,1)} %bitcast.102), calls=%async_computation.9 | async-start | bytes 2097152 | tf_op jit(solution)/shard_map/all_to_all | solution.py:100
  443.7 16.6 %collective-permute-start.50 = (bf16[1024,256]{1,0:T(8,128)(2,1)S(1)}, bf16[1024,256]{1,0:T(8,128)(2,1)S(1)}, u32[]{:S(2)}, u32[]{:S(2)}) collective-permute-start(bf16[1024,256]{1,0:T(8,128)(2,1)S(1)} %bitcast.100), channel_id=1, source_target_pairs={{0,2},{1,3},{2,0},{3,1},{4,6},{5,7},{6,4},{7,5},{8,10},{9,11},{10,... | collective-permute-start | bytes 1572872 | tf_op jit(solution)/shard_map/ppermute | solution.py:30
  449.1 54.9 %collective-permute-start.52 = (bf16[1024,1024]{1,0:T(8,128)(2,1)}, bf16[1024,1024]{1,0:T(8,128)(2,1)}, u32[]{:S(2)}, u32[]{:S(2)}) collective-permute-start(bf16[1024,1024]{1,0:T(8,128)(2,1)} %bitcast.32), channel_id=1, source_target_pairs={{0,4},{4,0},{1,5},{5,1},{2,6},{6,2},{3,7},{7,3},{8,12},{12,8},{9,1... | collective-permute-start | bytes 6291464 | tf_op jit(solution)/shard_map/ppermute | solution.py:30
  461.5 26.7 %collective-permute-start.51 = (bf16[1024,512]{1,0:T(8,128)(2,1)}, bf16[1024,512]{1,0:T(8,128)(2,1)}, u32[]{:S(2)}, u32[]{:S(2)}) collective-permute-start(bf16[1024,512]{1,0:T(8,128)(2,1)} %pad_maximum_fusion.1), channel_id=1, source_target_pairs={{0,1},{1,0},{2,3},{3,2},{4,5},{5,4},{6,7},{7,6},{8,9},{9,8},{10,11... | collective-permute-start | bytes 3145736 | tf_op jit(solution)/shard_map/ppermute | solution.py:30
  466.1 82.7 %collective-permute-start.53 = (bf16[1024,1024]{1,0:T(8,128)(2,1)S(1)}, bf16[1024,1024]{1,0:T(8,128)(2,1)}, u32[]{:S(2)}, u32[]{:S(2)}) collective-permute-start(bf16[1024,1024]{1,0:T(8,128)(2,1)S(1)} %bitcast.97), channel_id=1, source_target_pairs={{0,4},{4,0},{1,5},{5,1},{2,6},{6,2},{3,7},{7,3},{8,12},{12,8},{9,1... | collective-permute-start | bytes 6291464 | tf_op jit(solution)/shard_map/ppermute | solution.py:30
  471.1 12.9 %all-to-all-start.4 = ((bf16[256,4,128]{2,0,1:T(8,128)(2,1)}), bf16[256,4,128]{2,0,1:T(8,128)(2,1)S(1)}, u32[]{:S(2)}, u32[]{:S(2)}) async-start(bf16[256,4,128]{2,0,1:T(8,128)(2,1)} %copy_bitcast_fusion.2), calls=%async_computation.4 | async-start | bytes 524288 | tf_op jit(solution)/shard_map/all_to_all | solution.py:100
  484.0 24.5 %all-to-all-start.6 = ((bf16[256,4,256]{2,0,1:T(8,128)(2,1)}), bf16[256,4,256]{2,0,1:T(8,128)(2,1)}, u32[]{:S(2)}, u32[]{:S(2)}) async-start(bf16[256,4,256]{2,0,1:T(8,128)(2,1)} %add_convert_fusion), calls=%async_computation.6 | async-start | bytes 1048576 | tf_op jit(solution)/shard_map/all_to_all | solution.py:100
  (128 other events, 1142.9 us)

commit v2 on v1

--- a/solution.py
+++ b/solution.py
@@ -5,6 +5,7 @@
 
 D = 2048
 HD = 128
+
 
 epsilon = 1e-06
 rope_base = 500000.0
@@ -96,15 +97,72 @@
     return tensor
 
 
-def dp_share(tensor):
-    return lax.all_to_all(tensor, "dp", 1, 0, tiled=True)
-
-
-def dp_whole(tensor):
+def shifted(tensor, shift):
     size = lax.axis_size("dp")
-    spread = jnp.broadcast_to(tensor[None], (size,) + tensor.shape)
-    got = lax.all_to_all(spread, "dp", 0, 0, tiled=True)
-    return got.reshape((size * tensor.shape[0], tensor.shape[1]))
+    return lax.ppermute(tensor, "dp", [(i, (i + shift) % size) for i in range(size)])
+
+
+def dp_share(tensors):
+    size = lax.axis_size("dp")
+    me = lax.axis_index("dp")
+    widths = [tensor.shape[1] // size for tensor in tensors]
+
+    def cut(index):
+        return jnp.concatenate([share(t, index, w) for t, w in zip(tensors, widths)], 1)
+
+    blocks = [cut(me)]
+    for k in range(1, size):
+        blocks.append(shifted(cut((me + k) % size), k))
+    return blocks
+
+
+def dp_spread(tensor, relay=True):
+    size = lax.axis_size("dp")
+    blocks = [tensor]
+    if not relay or size > 4:
+        for k in range(1, size):
+            blocks.append(shifted(tensor, k))
+        return blocks
+    ups, downs = [tensor], [tensor]
+    for _ in range(1, size):
+        ups.append(lax.ppermute(ups[-1], "dp", [(i, i + 1) for i in range(size - 1)]))
+        downs.append(lax.ppermute(downs[-1], "dp", [(i + 1, i) for i in range(size - 1)]))
+    for k in range(1, size):
+        blocks.append(ups[k] + downs[size - k])
+    return blocks
+
+
+def columns(blocks, start, width):
+    return jnp.concatenate([block[:, start : start + width] for block in blocks], 0)
+
+
+def two_rows(left_own, left_other, right):
+    product = across_rows(left_other, right).astype(BF)
+    away = swap(product, "row", 1)
+    return across_rows(left_own, right), away
+
+
+def placed(own, away):
+    first = lax.axis_index("row") == 0
+    away = away.astype(F32)
+    return jnp.concatenate([jnp.where(first, own, away), jnp.where(first, away, own)], 1)
+
+
+def gain_totals(terms):
+    got = lax.all_gather(jnp.stack(terms), ("row", "col"))
+    rows, cols = lax.axis_size("row"), lax.axis_size("col")
+    got = got.reshape((rows, cols) + got.shape[1:])
+    by_head = jnp.swapaxes(got, 0, 1)
+    whole = jnp.stack(
+        [
+            by_head[:, :, 0].reshape(-1),
+            by_head[:, :, 1].reshape(-1),
+            got[:, :, 2].reshape(-1),
+            got[:, :, 3].reshape(-1),
+        ]
+    )
+    whole = sum(dp_spread(whole, relay=False))
+    return [whole[j] for j in range(4)]
 
 
 def rope_tables(row_count):
@@ -165,11 +223,7 @@
     return scale_rows * weighted - source * scale_rows**3 * stat_sum[:, None] / D
 
 
-def place_gain(term, offset):
-    return lax.dynamic_update_slice_in_dim(jnp.zeros((D,), F32), term, offset, 0)
-
-
-def body(
+def layer(
     hidden_in,
     seq_lengths,
     query_weight,
@@ -300,37 +354,43 @@
         "col",
     )
 
-    input_all = dp_share(input_block)
-    residual_all = dp_share(residual_block)
-    attended_all = dp_share(attended_rows)
-    hidden_all = dp_share(hidden_rows)
-    feed_all = gather(dp_whole(grad_feed.astype(BF)), "col")
-    gate_all = gather(dp_whole(grad_gate), "row")
-    up_all = gather(dp_whole(grad_up), "row")
-    mixer_all = gather(dp_whole(grad_mixer.astype(BF)), "col")
-    query_all = gather(dp_whole(grad_query), "row")
-    key_all = gather(dp_whole(grad_key), "row")
-    value_all = gather(dp_whole(grad_value_low), "row")
-    gain_sums = lax.psum(
-        (
-            place_gain(query_gain_term, head_start),
-            place_gain(key_gain_term, head_start),
-            place_gain(mixer_gain_term, feature_start),
-            place_gain(feed_gain_term, feature_start),
-        ),
-        ("dp", "row", "col"),
-    )
+    share_width = residual_block.shape[1] // lax.axis_size("dp")
+    cut = hidden_low.shape[1]
+    left_blocks = dp_share([input_block, residual_block, attended_rows])
+    left = columns(left_blocks, 0, 2 * share_width)
+    attended_all = columns(left_blocks, 2 * share_width, left_blocks[0].shape[1] - 2 * share_width)
+    other = swap(left, "row", 1)
+    hidden_all = jnp.concatenate(dp_share([hidden_rows]), 0)
+    feed_all = jnp.concatenate(dp_spread(grad_feed.astype(BF), relay=False), 0)
+    both_blocks = dp_spread(jnp.concatenate([grad_gate, grad_up], 1))
+    attention_blocks = dp_spread(
+        jnp.concatenate([grad_mixer.astype(BF), grad_query, grad_key, grad_value_low], 1),
+        relay=False,
+    )
+    mixer_all = columns(attention_blocks, 0, width)
+    attention_all = columns(attention_blocks, width, 3 * width)
+    feed_all = gather(feed_all, "col")
+    mixer_all = gather(mixer_all, "col")
+    gate_sum = placed(
+        *two_rows(left[:, share_width:], other[:, share_width:], columns(both_blocks, 0, cut))
+    )
+    up_sum = placed(
+        *two_rows(left[:, share_width:], other[:, share_width:], columns(both_blocks, cut, cut))
+    )
+    own, away = two_rows(left[:, :share_width], other[:, :share_width], attention_all)
+    attention_sums = [
+        placed(own[:, j * width : (j + 1) * width], away[:, j * width : (j + 1) * width])
+        for j in range(3)
+    ]
     return (
         block_out,
         grad_input.astype(BF),
-        across_rows(input_all, query_all),
-        across_rows(input_all, key_all),
-        across_rows(input_all, value_all),
+        *attention_sums,
         across_rows(attended_all, mixer_all),
-        across_rows(residual_all, gate_all),
-        across_rows(residual_all, up_all),
+        gate_sum,
+        up_sum,
         across_rows(hidden_all, feed_all),
-        *gain_sums,
+        *gain_totals([query_gain_term, key_gain_term, mixer_gain_term, feed_gain_term]),
     )
 
 
@@ -366,4 +426,4 @@
         P(),
         P(),
     )
-    return jax.shard_map(body, mesh=mesh, in_specs=in_specs, out_specs=out_specs, check_vma=False)
+    return jax.shard_map(layer, mesh=mesh, in_specs=in_specs, out_specs=out_specs, check_vma=False)

time: 556 us -> 481 us (0.87); the launches traced: 554 us -> 471 us
  blocking collectives: 126 us -> 10.9 us
  waiting for transfers between devices: 211 us -> 274 us
  matrix products: 46.3 us -> 28.9 us
  starting transfers between devices: 98.3 us -> 92 us
    ppermute x0 -> x21, waiting for transfers between devices: none -> 123 us  [the longest x15 90.2 us: shifted(): lax.ppermute(tensor, 'dp', [(i, (i + shift) % size) for i in range(size)])]
    all_to_all x2 -> x0, blocking collectives: 66 us -> none  [dp_whole(): got = lax.all_to_all(spread, 'dp', 0, 0, tiled=True)]
    psum x1 -> x0, blocking collectives: 59.9 us -> none  [body(): lax.psum((place_gain(query_gain_term, head_start), place_gain(key_gain_te...]
    ppermute x0 -> x21, starting transfers between devices: none -> 41.9 us  [the longest x15 24.1 us: shifted(): lax.ppermute(tensor, 'dp', [(i, (i + shift) % size) for i in range(size)])]
    all_to_all x9 -> x0, starting transfers between devices: 37.7 us -> none  [the longest x5 20.6 us: dp_whole(): got = lax.all_to_all(spread, 'dp', 0, 0, tiled=True)]
    all_to_all x9 -> x0, waiting for transfers between devices: 31.2 us -> none  [the longest x5 26.4 us: dp_whole(): got = lax.all_to_all(spread, 'dp', 0, 0, tiled=True)]
    ppermute x56 -> x55, waiting for transfers between devices: 180 us -> 151 us  [swap(): return lax.ppermute(tensor, axis, [(i, i ^ bit) for i in range(size)])]
    select_n x19 -> x14, other arithmetic: 20.5 us -> 3.29 us  [ordered(): moved[j] = jnp.where(flip, pieces[j | bit], pieces[j])]
  transfers between devices with their start and end apart: 65 -> 76, of which waited for: 46 -> 44; matrix products, arithmetic and copies ran while one was open for 15% -> 12% of each run, Pallas kernels for 0% -> 0%
where the time goes in v2:
time: 481 us; the launch traced here: 471 us
  waiting for transfers between devices  274 us (57%)
  starting transfers between devices  92 us (19%)
  other arithmetic  45.4 us (9%)
  matrix products  28.9 us (6%)
  local copies, waits for them, and re-layouts  16 us (3%)
  blocking collectives  10.9 us (2%)
    ppermute x55, waiting for transfers between devices, swap(): return lax.ppermute(tensor, axis, [(i, i ^ bit) for i in range(size)])  151 us
    ppermute x15, waiting for transfers between devices, shifted(): lax.ppermute(tensor, 'dp', [(i, (i + shift) % size) for i in range(size)])  90.2 us
    ppermute x55, starting transfers between devices, swap(): return lax.ppermute(tensor, axis, [(i, i ^ bit) for i in range(size)])  50 us
    ppermute x3, waiting for transfers between devices, dp_spread(): lax.ppermute(ups[-1], 'dp', [(i, i + 1) for i in range(size - 1)])  26.9 us
    ppermute x15, starting transfers between devices, shifted(): lax.ppermute(tensor, 'dp', [(i, (i + shift) % size) for i in range(size)])  24.1 us
    ppermute x3, starting transfers between devices, dp_spread(): lax.ppermute(ups[-1], 'dp', [(i, i + 1) for i in range(size - 1)])  13.7 us
    dot_general x11, matrix products, mul_f32(): return jnp.dot(left, right, preferred_element_type=F32)  11.6 us
    all_gather x1, blocking collectives, gain_totals(): got = lax.all_gather(jnp.stack(terms), ('row', 'col'))  10.9 us
  transfers between devices with their start and end apart: 76, of which 44 were waited for; matrix products, arithmetic and copies ran while one was open for 12% of the time, Pallas kernels for 0%

profile of v2, /device:TPU:0, one launch (start us, length us, event | category | flops | bytes accessed | tf_op | source)
XLA Modules:
  0.0 471.3 jit_solution(15841466842806082910)
XLA Ops:
  0.7 3.0 collective-permute-start
  3.7 3.7 collective-permute-done
  18.8 4.1 collective-permute-done.3
  24.0 3.6 collective-permute-done.2
  44.9 3.4 collective-permute-done.8
  53.0 4.2 collective-permute-done.10
  59.8 3.5 collective-permute-done.14
  66.3 2.1 collective-permute-done.12
  70.0 2.0 collective-permute-done.13
  74.1 3.7 fusion.190
  81.5 11.3 %collective-permute-done.17 = bf16[256,1024]{1,0:T(8,128)(2,1)S(1)} collective-permute-done((bf16[256,1024]{1,0:T(8,128)(2,1)S(1)}, bf16[256,1024]{1,0:T(8,128)(2,1)S(1)}, u32[]{:S(2)}, u32[]{:S(2)}) %collective-permute-start.17) | collective-permute-done | bytes 524320 | tf_op jit(solution)/shard_map/ppermute | solution.py:31
  92.8 8.3 %collective-permute-done.16 = bf16[256,1024]{1,0:T(8,128)(2,1)S(1)} collective-permute-done((bf16[256,1024]{1,0:T(8,128)(2,1)S(1)}, bf16[256,1024]{1,0:T(8,128)(2,1)S(1)}, u32[]{:S(2)}, u32[]{:S(2)}) %collective-permute-start.16) | collective-permute-done | bytes 524320 | tf_op jit(solution)/shard_map/ppermute | solution.py:31
  103.1 9.5 %collective-permute-done.18 = bf16[256,1024]{1,0:T(8,128)(2,1)S(1)} collective-permute-done((bf16[256,1024]{1,0:T(8,128)(2,1)S(1)}, bf16[256,1024]{1,0:T(8,128)(2,1)S(1)}, u32[]{:S(2)}, u32[]{:S(2)}) %collective-permute-start.18) | collective-permute-done | bytes 524320 | tf_op jit(solution)/shard_map/ppermute | solution.py:31
  118.5 4.4 collective-permute-done.20
  138.4 2.1 collective-permute-start.28
  141.3 11.7 %collective-permute-done.28 = bf16[256,1024]{1,0:T(8,128)(2,1)} collective-permute-done((bf16[256,1024]{1,0:T(8,128)(2,1)S(1)}, bf16[256,1024]{1,0:T(8,128)(2,1)}, u32[]{:S(2)}, u32[]{:S(2)}) %collective-permute-start.28) | collective-permute-done | bytes 524320 | tf_op jit(solution)/shard_map/ppermute | solution.py:31
  153.0 3.0 multiply_convert_fusion.1
  160.5 10.4 %collective-permute-done.30 = bf16[256,1024]{1,0:T(8,128)(2,1)S(1)} collective-permute-done((bf16[256,1024]{1,0:T(8,128)(2,1)S(1)}, bf16[256,1024]{1,0:T(8,128)(2,1)S(1)}, u32[]{:S(2)}, u32[]{:S(2)}) %collective-permute-start.30) | collective-permute-done | bytes 524320 | tf_op jit(solution)/shard_map/ppermute | solution.py:31
  172.3 8.2 %collective-permute-done.29 = bf16[256,1024]{1,0:T(8,128)(2,1)S(1)} collective-permute-done((bf16[256,1024]{1,0:T(8,128)(2,1)S(1)}, bf16[256,1024]{1,0:T(8,128)(2,1)S(1)}, u32[]{:S(2)}, u32[]{:S(2)}) %collective-permute-start.29) | collective-permute-done | bytes 524320 | tf_op jit(solution)/shard_map/ppermute | solution.py:31
  182.1 3.6 collective-permute-start.49
  189.8 4.1 collective-permute-done.49
  194.0 20.4 %collective-permute-done.48 = bf16[256,640]{1,0:T(8,128)(2,1)S(1)} collective-permute-done((bf16[256,640]{1,0:T(8,128)(2,1)S(1)}, bf16[256,640]{1,0:T(8,128)(2,1)S(1)}, u32[]{:S(2)}, u32[]{:S(2)}) %collective-permute-start.48) | collective-permute-done | bytes 327712 | tf_op jit(solution)/shard_map/ppermute | solution.py:102
  218.8 2.8 collective-permute-done.33
  225.8 2.9 collective-permute-start.69
  228.7 2.0 collective-permute-start.68
  232.9 8.0 %collective-permute-done.69 = bf16[256,256]{1,0:T(8,128)(2,1)S(1)} collective-permute-done((bf16[256,256]{1,0:T(8,128)(2,1)S(1)}, bf16[256,256]{1,0:T(8,128)(2,1)S(1)}, u32[]{:S(2)}, u32[]{:S(2)}) %collective-permute-start.69) | collective-permute-done | bytes 131104 | tf_op jit(solution)/shard_map/ppermute | solution.py:102
  248.7 10.9 %all-gather.1 = f32[8,4,256]{2,1,0:T(4,128)S(1)} all-gather(f32[1,4,256]{2,1,0:T(4,128)S(1)} %maximum_bitcast_fusion), channel_id=2, replica_groups=mesh['dp'=4,'row'=2,'col'=4] {'row','col'}, dimensions={0}, use_global_device_ids=true | all-gather | bytes 36864 | tf_op jit(solution)/shard_map/all_gather | solution.py:152
  260.8 2.4 collective-permute-done.40
  268.4 2.0 constant_dynamic-update-slice_fusion.3
  280.4 5.2 %collective-permute-done.43 = bf16[256,256]{1,0:T(8,128)(2,1)S(1)} collective-permute-done((bf16[256,256]{1,0:T(8,128)(2,1)S(1)}, bf16[256,256]{1,0:T(8,128)(2,1)S(1)}, u32[]{:S(2)}, u32[]{:S(2)}) %collective-permute-start.43) | collective-permute-done | bytes 131104 | tf_op jit(solution)/shard_map/ppermute | solution.py:31
  286.1 5.4 %collective-permute-done.42 = bf16[256,256]{1,0:T(8,128)(2,1)S(1)} collective-permute-done((bf16[256,256]{1,0:T(8,128)(2,1)S(1)}, bf16[256,256]{1,0:T(8,128)(2,1)S(1)}, u32[]{:S(2)}, u32[]{:S(2)}) %collective-permute-start.42) | collective-permute-done | bytes 131104 | tf_op jit(solution)/shard_map/ppermute | solution.py:31
  293.1 4.0 collective-permute-start.57
  300.0 2.2 collective-permute-start.51
  302.2 4.0 collective-permute-done.52
  307.0 53.6 %collective-permute-done.51 = bf16[256,1024]{1,0:T(8,128)(2,1)S(1)} collective-permute-done((bf16[256,1024]{1,0:T(8,128)(2,1)S(1)}, bf16[256,1024]{1,0:T(8,128)(2,1)S(1)}, u32[]{:S(2)}, u32[]{:S(2)}) %collective-permute-start.51) | collective-permute-done | bytes 524320 | tf_op jit(solution)/shard_map/ppermute | solution.py:102
  360.8 4.0 collective-permute-start.61
  368.2 3.1 collective-permute-done.46
  371.2 2.8 collective-permute-start.54
  374.8 10.3 %collective-permute-done.61 = bf16[256,2048]{1,0:T(8,128)(2,1)S(1)} collective-permute-done((bf16[256,2048]{1,0:T(8,128)(2,1)S(1)}, bf16[256,2048]{1,0:T(8,128)(2,1)S(1)}, u32[]{:S(2)}, u32[]{:S(2)}) %collective-permute-start.61) | collective-permute-done | bytes 1048608 | tf_op jit(solution)/shard_map/ppermute | solution.py:128
  385.1 9.5 %collective-permute-start.65 = (bf16[256,512]{1,0:T(8,128)(2,1)S(1)}, bf16[256,512]{1,0:T(8,128)(2,1)S(1)}, u32[]{:S(2)}, u32[]{:S(2)}) collective-permute-start(bf16[256,512]{1,0:T(8,128)(2,1)S(1)} %copy-done.62), channel_id=1, source_target_pairs={{0,8},{8,16},{16,24},{24,0},{1,9},{9,17},{17,25},{25,1},{2,10},{10... | collective-permute-start | bytes 786440 | tf_op jit(solution)/shard_map/ppermute | solution.py:102
  400.1 11.1 %collective-permute-done.55 = bf16[1024,256]{1,0:T(8,128)(2,1)S(1)} collective-permute-done((bf16[1024,256]{1,0:T(8,128)(2,1)S(1)}, bf16[1024,256]{1,0:T(8,128)(2,1)S(1)}, u32[]{:S(2)}, u32[]{:S(2)}) %collective-permute-start.55) | collective-permute-done | bytes 524320 | tf_op jit(solution)/shard_map/ppermute | solution.py:31
  411.2 5.7 %collective-permute-start.62 = (bf16[256,2048]{1,0:T(8,128)(2,1)S(1)}, bf16[256,2048]{1,0:T(8,128)(2,1)S(1)}, u32[]{:S(2)}, u32[]{:S(2)}) collective-permute-start(bf16[256,2048]{1,0:T(8,128)(2,1)S(1)} %collective-permute-done.61), channel_id=1, source_target_pairs={{0,8},{8,16},{16,24},{1,9},{9,17},{17,25},{2,10},{10,18},{18,26},{... | collective-permute-start | bytes 3145736 | tf_op jit(solution)/shard_map/ppermute | solution.py:128
  419.9 2.6 fusion.8
  422.5 16.6 %collective-permute-done.62 = bf16[256,2048]{1,0:T(8,128)(2,1)S(1)} collective-permute-done((bf16[256,2048]{1,0:T(8,128)(2,1)S(1)}, bf16[256,2048]{1,0:T(8,128)(2,1)S(1)}, u32[]{:S(2)}, u32[]{:S(2)}) %collective-permute-start.62) | collective-permute-done | bytes 1048608 | tf_op jit(solution)/shard_map/ppermute | solution.py:128
  439.6 3.8 collective-permute-done.60
  444.6 2.3 collective-permute-start.63
  450.4 9.3 %collective-permute-done.63 = bf16[256,1024]{1,0:T(8,128)(2,1)S(1)} collective-permute-done((bf16[256,1024]{1,0:T(8,128)(2,1)S(1)}, bf16[256,1024]{1,0:T(8,128)(2,1)S(1)}, u32[]{:S(2)}, u32[]{:S(2)}) %collective-permute-start.63) | collective-permute-done | bytes 524320 | tf_op jit(solution)/shard_map/ppermute | solution.py:31
  461.9 6.8 %collective-permute-done.64 = bf16[256,1024]{1,0:T(8,128)(2,1)S(1)} collective-permute-done((bf16[256,1024]{1,0:T(8,128)(2,1)S(1)}, bf16[256,1024]{1,0:T(8,128)(2,1)S(1)}, u32[]{:S(2)}, u32[]{:S(2)}) %collective-permute-start.64) | collective-permute-done | bytes 524320 | tf_op jit(solution)/shard_map/ppermute | solution.py:31
  (535 shorter events, 143.7 us)
Async XLA Ops:
  0.7 6.7 %collective-permute-start = (bf16[256,256]{1,0:T(8,128)(2,1)}, bf16[256,256]{1,0:T(8,128)(2,1)S(1)}, u32[]{:S(2)}, u32[]{:S(2)}) collective-permute-start(bf16[256,256]{1,0:T(8,128)(2,1)} %param.14), channel_id=1, source_target_pairs={{0,2},{1,3},{2,0},{3,1},{4,6},{5,7},{6,4},{7,5},{8,10},{9,11},{10,... | collective-permute-start | bytes 393224 | tf_op jit(solution)/shard_map/ppermute | solution.py:31
  13.6 9.3 %collective-permute-start.3 = (f32[256,256]{1,0:T(8,128)S(1)}, f32[256,256]{1,0:T(8,128)}, u32[]{:S(2)}, u32[]{:S(2)}) collective-permute-start(f32[256,256]{1,0:T(8,128)S(1)} %constant_dynamic-slice_fusion.8), channel_id=1, source_target_pairs={{0,4},{4,0},{1,5},{5,1},{2,6},{6,2},{3,7},{7,3},{8,12},{12,8},{9,1... | collective-permute-start | bytes 786440 | tf_op jit(solution)/shard_map/ppermute | solution.py:31
  15.8 11.7 %collective-permute-start.2 = (f32[256,256]{1,0:T(8,128)S(1)}, f32[256,256]{1,0:T(8,128)S(1)}, u32[]{:S(2)}, u32[]{:S(2)}) collective-permute-start(f32[256,256]{1,0:T(8,128)S(1)} %constant_dynamic-slice_fusion.9), channel_id=1, source_target_pairs={{0,4},{4,0},{1,5},{5,1},{2,6},{6,2},{3,7},{7,3},{8,12},{12,8},{9,1... | collective-permute-start | bytes 786440 | tf_op jit(solution)/shard_map/ppermute | solution.py:31
  63.3 9.3 %collective-permute-start.15 = (bf16[256,512]{1,0:T(8,128)(2,1)S(1)}, bf16[256,512]{1,0:T(8,128)(2,1)S(1)}, u32[]{:S(2)}, u32[]{:S(2)}) collective-permute-start(bf16[256,512]{1,0:T(8,128)(2,1)S(1)} %pad_maximum_fusion.29), channel_id=1, source_target_pairs={{0,1},{1,0},{2,3},{3,2},{4,5},{5,4},{6,7},{7,6},{8,9},{9,8},{10,11... | collective-permute-start | bytes 786440 | tf_op jit(solution)/shard_map/ppermute | solution.py:31
  78.0 14.9 %collective-permute-start.17 = (bf16[256,1024]{1,0:T(8,128)(2,1)S(1)}, bf16[256,1024]{1,0:T(8,128)(2,1)S(1)}, u32[]{:S(2)}, u32[]{:S(2)}) collective-permute-start(bf16[256,1024]{1,0:T(8,128)(2,1)S(1)} %dynamic-slice_convert_fusion.1), channel_id=1, source_target_pairs={{0,4},{4,0},{1,5},{5,1},{2,6},{6,2},{3,7},{7,3},{8,12},{12,8},{9,1... | collective-permute-start | bytes 1572872 | tf_op jit(solution)/shard_map/ppermute | solution.py:31
  80.9 20.2 %collective-permute-start.16 = (bf16[256,1024]{1,0:T(8,128)(2,1)S(1)}, bf16[256,1024]{1,0:T(8,128)(2,1)S(1)}, u32[]{:S(2)}, u32[]{:S(2)}) collective-permute-start(bf16[256,1024]{1,0:T(8,128)(2,1)S(1)} %dynamic-slice_convert_fusion.2), channel_id=1, source_target_pairs={{0,4},{4,0},{1,5},{5,1},{2,6},{6,2},{3,7},{7,3},{8,12},{12,8},{9,1... | collective-permute-start | bytes 1572872 | tf_op jit(solution)/shard_map/ppermute | solution.py:31
  101.5 11.1 %collective-permute-start.18 = (bf16[256,1024]{1,0:T(8,128)(2,1)S(1)}, bf16[256,1024]{1,0:T(8,128)(2,1)S(1)}, u32[]{:S(2)}, u32[]{:S(2)}) collective-permute-start(bf16[256,1024]{1,0:T(8,128)(2,1)S(1)} %multiply_convert_fusion.2), channel_id=1, source_target_pairs={{0,4},{4,0},{1,5},{5,1},{2,6},{6,2},{3,7},{7,3},{8,12},{12,8},{9,1... | collective-permute-start | bytes 1572872 | tf_op jit(solution)/shard_map/ppermute | solution.py:31
  116.4 6.5 %collective-permute-start.20 = (bf16[256,256]{1,0:T(8,128)(2,1)S(1)}, bf16[256,256]{1,0:T(8,128)(2,1)}, u32[]{:S(2)}, u32[]{:S(2)}) collective-permute-start(bf16[256,256]{1,0:T(8,128)(2,1)S(1)} %add_convert_fusion.5), channel_id=1, source_target_pairs={{0,2},{1,3},{2,0},{3,1},{4,6},{5,7},{6,4},{7,5},{8,10},{9,11},{10,... | collective-permute-start | bytes 393224 | tf_op jit(solution)/shard_map/ppermute | solution.py:31
  117.9 7.0 %collective-permute-start.24 = (bf16[256,256]{1,0:T(8,128)(2,1)S(1)}, bf16[256,256]{1,0:T(8,128)(2,1)}, u32[]{:S(2)}, u32[]{:S(2)}) collective-permute-start(bf16[256,256]{1,0:T(8,128)(2,1)S(1)} %copy-done.8), channel_id=1, source_target_pairs={{0,2},{1,3},{2,0},{3,1},{4,6},{5,7},{6,4},{7,5},{8,10},{9,11},{10,... | collective-permute-start | bytes 393224 | tf_op jit(solution)/shard_map/ppermute | solution.py:31
  138.4 14.6 %collective-permute-start.28 = (bf16[256,1024]{1,0:T(8,128)(2,1)S(1)}, bf16[256,1024]{1,0:T(8,128)(2,1)}, u32[]{:S(2)}, u32[]{:S(2)}) collective-permute-start(bf16[256,1024]{1,0:T(8,128)(2,1)S(1)} %dynamic-slice_convert_fusion), channel_id=1, source_target_pairs={{0,4},{4,0},{1,5},{5,1},{2,6},{6,2},{3,7},{7,3},{8,12},{12,8},{9,1... | collective-permute-start | bytes 1572872 | tf_op jit(solution)/shard_map/ppermute | solution.py:31
  156.1 14.9 %collective-permute-start.30 = (bf16[256,1024]{1,0:T(8,128)(2,1)S(1)}, bf16[256,1024]{1,0:T(8,128)(2,1)S(1)}, u32[]{:S(2)}, u32[]{:S(2)}) collective-permute-start(bf16[256,1024]{1,0:T(8,128)(2,1)S(1)} %get-tuple-element.39), channel_id=1, source_target_pairs={{0,4},{4,0},{1,5},{5,1},{2,6},{6,2},{3,7},{7,3},{8,12},{12,8},{9,1... | collective-permute-start | bytes 1572872 | tf_op jit(solution)/shard_map/ppermute | solution.py:31
  159.9 20.5 %collective-permute-start.29 = (bf16[256,1024]{1,0:T(8,128)(2,1)S(1)}, bf16[256,1024]{1,0:T(8,128)(2,1)S(1)}, u32[]{:S(2)}, u32[]{:S(2)}) collective-permute-start(bf16[256,1024]{1,0:T(8,128)(2,1)S(1)} %get-tuple-element.38), channel_id=1, source_target_pairs={{0,4},{4,0},{1,5},{5,1},{2,6},{6,2},{3,7},{7,3},{8,12},{12,8},{9,1... | collective-permute-start | bytes 1572872 | tf_op jit(solution)/shard_map/ppermute | solution.py:31
  182.1 11.8 %collective-permute-start.49 = (bf16[256,640]{1,0:T(8,128)(2,1)S(1)}, bf16[256,640]{1,0:T(8,128)(2,1)S(1)}, u32[]{:S(2)}, u32[]{:S(2)}) collective-permute-start(bf16[256,640]{1,0:T(8,128)(2,1)S(1)} %pad_maximum_fusion.25), channel_id=1, source_target_pairs={{0,24},{8,0},{16,8},{24,16},{1,25},{9,1},{17,9},{25,17},{2,26},{10... | collective-permute-start | bytes 983048 | tf_op jit(solution)/shard_map/ppermute | solution.py:102
  185.8 28.6 %collective-permute-start.48 = (bf16[256,640]{1,0:T(8,128)(2,1)S(1)}, bf16[256,640]{1,0:T(8,128)(2,1)S(1)}, u32[]{:S(2)}, u32[]{:S(2)}) collective-permute-start(bf16[256,640]{1,0:T(8,128)(2,1)S(1)} %pad_maximum_fusion.24), channel_id=1, source_target_pairs={{0,16},{8,24},{16,0},{24,8},{1,17},{9,25},{17,1},{25,9},{2,18},{10... | collective-permute-start | bytes 983048 | tf_op jit(solution)/shard_map/ppermute | solution.py:102
  185.9 28.5 %collective-permute-start.47 = (bf16[256,640]{1,0:T(8,128)(2,1)S(1)}, bf16[256,640]{1,0:T(8,128)(2,1)S(1)}, u32[]{:S(2)}, u32[]{:S(2)}) collective-permute-start(bf16[256,640]{1,0:T(8,128)(2,1)S(1)} %pad_maximum_fusion.23), channel_id=1, source_target_pairs={{0,8},{8,16},{16,24},{24,0},{1,9},{9,17},{17,25},{25,1},{2,10},{10... | collective-permute-start | bytes 983048 | tf_op jit(solution)/shard_map/ppermute | solution.py:102
  187.0 27.4 %collective-permute-start.32 = (bf16[256,256]{1,0:T(8,128)(2,1)S(1)}, bf16[256,256]{1,0:T(8,128)(2,1)S(1)}, u32[]{:S(2)}, u32[]{:S(2)}) collective-permute-start(bf16[256,256]{1,0:T(8,128)(2,1)S(1)} %add_convert_fusion.3), channel_id=1, source_target_pairs={{0,2},{1,3},{2,0},{3,1},{4,6},{5,7},{6,4},{7,5},{8,10},{9,11},{10,... | collective-permute-start | bytes 393224 | tf_op jit(solution)/shard_map/ppermute | solution.py:31
  215.5 6.0 %collective-permute-start.33 = (bf16[256,256]{1,0:T(8,128)(2,1)S(1)}, bf16[256,256]{1,0:T(8,128)(2,1)S(1)}, u32[]{:S(2)}, u32[]{:S(2)}) collective-permute-start(bf16[256,256]{1,0:T(8,128)(2,1)S(1)} %convert_element_type.259), channel_id=1, source_target_pairs={{0,2},{1,3},{2,0},{3,1},{4,6},{5,7},{6,4},{7,5},{8,10},{9,11},{10,... | collective-permute-start | bytes 393224 | tf_op jit(solution)/shard_map/ppermute | solution.py:31
  221.5 9.2 %collective-permute-start.34 = (bf16[256,512]{1,0:T(8,128)(2,1)S(1)}, bf16[256,512]{1,0:T(8,128)(2,1)S(1)}, u32[]{:S(2)}, u32[]{:S(2)}) collective-permute-start(bf16[256,512]{1,0:T(8,128)(2,1)S(1)} %pad_maximum_fusion.34), channel_id=1, source_target_pairs={{0,1},{1,0},{2,3},{3,2},{4,5},{5,4},{6,7},{7,6},{8,9},{9,8},{10,11... | collective-permute-start | bytes 786440 | tf_op jit(solution)/shard_map/ppermute | solution.py:31
  223.2 7.5 %collective-permute-start.37 = (f32[256]{0:T(256)S(1)}, f32[256]{0:T(256)S(1)}, u32[]{:S(2)}, u32[]{:S(2)}) collective-permute-start(f32[256]{0:T(256)S(1)} %add.389), channel_id=1, source_target_pairs={{0,4},{4,0},{1,5},{5,1},{2,6},{6,2},{3,7},{7,3},{8,12},{12,8},{9,1... | collective-permute-start | bytes 3080 | tf_op jit(solution)/shard_map/ppermute | solution.py:31
  225.8 7.1 %collective-permute-start.70 = (bf16[256,256]{1,0:T(8,128)(2,1)S(1)}, bf16[256,256]{1,0:T(8,128)(2,1)S(1)}, u32[]{:S(2)}, u32[]{:S(2)}) collective-permute-start(bf16[256,256]{1,0:T(8,128)(2,1)S(1)} %get-tuple-element.111), channel_id=1, source_target_pairs={{0,24},{8,0},{16,8},{24,16},{1,25},{9,1},{17,9},{25,17},{2,26},{10... | collective-permute-start | bytes 393224 | tf_op jit(solution)/shard_map/ppermute | solution.py:102
  225.8 15.1 %collective-permute-start.69 = (bf16[256,256]{1,0:T(8,128)(2,1)S(1)}, bf16[256,256]{1,0:T(8,128)(2,1)S(1)}, u32[]{:S(2)}, u32[]{:S(2)}) collective-permute-start(bf16[256,256]{1,0:T(8,128)(2,1)S(1)} %get-tuple-element.111), channel_id=1, source_target_pairs={{0,16},{8,24},{16,0},{24,8},{1,17},{9,25},{17,1},{25,9},{2,18},{10... | collective-permute-start | bytes 393224 | tf_op jit(solution)/shard_map/ppermute | solution.py:102
  228.7 12.3 %collective-permute-start.68 = (bf16[256,256]{1,0:T(8,128)(2,1)S(1)}, bf16[256,256]{1,0:T(8,128)(2,1)S(1)}, u32[]{:S(2)}, u32[]{:S(2)}) collective-permute-start(bf16[256,256]{1,0:T(8,128)(2,1)S(1)} %get-tuple-element.111), channel_id=1, source_target_pairs={{0,8},{8,16},{16,24},{24,0},{1,9},{9,17},{17,25},{25,1},{2,10},{10... | collective-permute-start | bytes 393224 | tf_op jit(solution)/shard_map/ppermute | solution.py:102
  231.5 11.8 %collective-permute-start.38 = (bf16[256,256]{1,0:T(8,128)(2,1)S(1)}, bf16[256,256]{1,0:T(8,128)(2,1)S(1)}, u32[]{:S(2)}, u32[]{:S(2)}) collective-permute-start(bf16[256,256]{1,0:T(8,128)(2,1)S(1)} %dynamic-slice_convert_fusion.5), channel_id=1, source_target_pairs={{0,4},{4,0},{1,5},{5,1},{2,6},{6,2},{3,7},{7,3},{8,12},{12,8},{9,1... | collective-permute-start | bytes 393224 | tf_op jit(solution)/shard_map/ppermute | solution.py:31
  241.8 56.6 %collective-permute-start.71 = (bf16[1024,256]{1,0:T(8,128)(2,1)}, bf16[1024,256]{1,0:T(8,128)(2,1)S(1)}, u32[]{:S(2)}, u32[]{:S(2)}) collective-permute-start(bf16[1024,256]{1,0:T(8,128)(2,1)} %pad_maximum_fusion.17), channel_id=1, source_target_pairs={{0,2},{1,3},{2,0},{3,1},{4,6},{5,7},{6,4},{7,5},{8,10},{9,11},{10,... | collective-permute-start | bytes 1572872 | tf_op jit(solution)/shard_map/ppermute | solution.py:31
  248.6 11.0 %collective-permute-start.39 = (f32[2,256]{1,0:T(2,128)S(1)}, f32[2,256]{1,0:T(2,128)S(1)}, u32[]{:S(2)}, u32[]{:S(2)}) collective-permute-start(f32[2,256]{1,0:T(2,128)S(1)} %pad_maximum_fusion.56), channel_id=1, source_target_pairs={{0,1},{1,0},{2,3},{3,2},{4,5},{5,4},{6,7},{7,6},{8,9},{9,8},{10,11... | collective-permute-start | bytes 6152 | tf_op jit(solution)/shard_map/ppermute | solution.py:31
  274.9 17.3 %collective-permute-start.75 = (f32[4,2048]{1,0:T(4,128)S(1)}, f32[4,2048]{1,0:T(4,128)S(1)}, u32[]{:S(2)}, u32[]{:S(2)}) collective-permute-start(f32[4,2048]{1,0:T(4,128)S(1)} %pad_maximum_fusion.45), channel_id=1, source_target_pairs={{0,24},{8,0},{16,8},{24,16},{1,25},{9,1},{17,9},{25,17},{2,26},{10... | collective-permute-start | bytes 98312 | tf_op jit(solution)/shard_map/ppermute | solution.py:102
  275.1 17.7 %collective-permute-start.74 = (f32[4,2048]{1,0:T(4,128)S(1)}, f32[4,2048]{1,0:T(4,128)S(1)}, u32[]{:S(2)}, u32[]{:S(2)}) collective-permute-start(f32[4,2048]{1,0:T(4,128)S(1)} %pad_maximum_fusion.45), channel_id=1, source_target_pairs={{0,16},{8,24},{16,0},{24,8},{1,17},{9,25},{17,1},{25,9},{2,18},{10... | collective-permute-start | bytes 98312 | tf_op jit(solution)/shard_map/ppermute | solution.py:102
  275.7 21.4 %collective-permute-start.73 = (f32[4,2048]{1,0:T(4,128)S(1)}, f32[4,2048]{1,0:T(4,128)S(1)}, u32[]{:S(2)}, u32[]{:S(2)}) collective-permute-start(f32[4,2048]{1,0:T(4,128)S(1)} %pad_maximum_fusion.45), channel_id=1, source_target_pairs={{0,8},{8,16},{16,24},{24,0},{1,9},{9,17},{17,25},{25,1},{2,10},{10... | collective-permute-start | bytes 98312 | tf_op jit(solution)/shard_map/ppermute | solution.py:102
  279.2 6.4 %collective-permute-start.43 = (bf16[256,256]{1,0:T(8,128)(2,1)S(1)}, bf16[256,256]{1,0:T(8,128)(2,1)S(1)}, u32[]{:S(2)}, u32[]{:S(2)}) collective-permute-start(bf16[256,256]{1,0:T(8,128)(2,1)S(1)} %get-tuple-element.22), channel_id=1, source_target_pairs={{0,4},{4,0},{1,5},{5,1},{2,6},{6,2},{3,7},{7,3},{8,12},{12,8},{9,1... | collective-permute-start | bytes 393224 | tf_op jit(solution)/shard_map/ppermute | solution.py:31
  291.5 14.7 %collective-permute-start.52 = (bf16[256,1024]{1,0:T(8,128)(2,1)S(1)}, bf16[256,1024]{1,0:T(8,128)(2,1)S(1)}, u32[]{:S(2)}, u32[]{:S(2)}) collective-permute-start(bf16[256,1024]{1,0:T(8,128)(2,1)S(1)} %copy-done.90), channel_id=1, source_target_pairs={{0,24},{8,0},{16,8},{24,16},{1,25},{9,1},{17,9},{25,17},{2,26},{10... | collective-permute-start | bytes 1572872 | tf_op jit(solution)/shard_map/ppermute | solution.py:102
  292.8 73.4 %collective-permute-start.53 = (bf16[1024,512]{1,0:T(8,128)(2,1)S(1)}, bf16[1024,512]{1,0:T(8,128)(2,1)S(1)}, u32[]{:S(2)}, u32[]{:S(2)}) collective-permute-start(bf16[1024,512]{1,0:T(8,128)(2,1)S(1)} %copy-done.46), channel_id=1, source_target_pairs={{0,4},{4,0},{1,5},{5,1},{2,6},{6,2},{3,7},{7,3},{8,12},{12,8},{9,1... | collective-permute-start | bytes 3145736 | tf_op jit(solution)/shard_map/ppermute | solution.py:31
  293.1 67.6 %collective-permute-start.57 = (bf16[256,2048]{1,0:T(8,128)(2,1)S(1)}, bf16[256,2048]{1,0:T(8,128)(2,1)S(1)}, u32[]{:S(2)}, u32[]{:S(2)}) collective-permute-start(bf16[256,2048]{1,0:T(8,128)(2,1)S(1)} %copy-done.47), channel_id=1, source_target_pairs={{0,8},{8,16},{16,24},{1,9},{9,17},{17,25},{2,10},{10,18},{18,26},{... | collective-permute-start | bytes 3145736 | tf_op jit(solution)/shard_map/ppermute | solution.py:128
  297.1 63.7 %collective-permute-start.58 = (bf16[256,2048]{1,0:T(8,128)(2,1)S(1)}, bf16[256,2048]{1,0:T(8,128)(2,1)S(1)}, u32[]{:S(2)}, u32[]{:S(2)}) collective-permute-start(bf16[256,2048]{1,0:T(8,128)(2,1)S(1)} %copy-done.47), channel_id=1, source_target_pairs={{8,0},{16,8},{24,16},{9,1},{17,9},{25,17},{10,2},{18,10},{26,18},{... | collective-permute-start | bytes 3145736 | tf_op jit(solution)/shard_map/ppermute | solution.py:129
  300.0 60.7 %collective-permute-start.51 = (bf16[256,1024]{1,0:T(8,128)(2,1)S(1)}, bf16[256,1024]{1,0:T(8,128)(2,1)S(1)}, u32[]{:S(2)}, u32[]{:S(2)}) collective-permute-start(bf16[256,1024]{1,0:T(8,128)(2,1)S(1)} %copy-done.90), channel_id=1, source_target_pairs={{0,16},{8,24},{16,0},{24,8},{1,17},{9,25},{17,1},{25,9},{2,18},{10... | collective-permute-start | bytes 1572872 | tf_op jit(solution)/shard_map/ppermute | solution.py:102
  306.2 58.6 %collective-permute-start.50 = (bf16[256,1024]{1,0:T(8,128)(2,1)S(1)}, bf16[256,1024]{1,0:T(8,128)(2,1)S(1)}, u32[]{:S(2)}, u32[]{:S(2)}) collective-permute-start(bf16[256,1024]{1,0:T(8,128)(2,1)S(1)} %copy-done.90), channel_id=1, source_target_pairs={{0,8},{8,16},{16,24},{24,0},{1,9},{9,17},{17,25},{25,1},{2,10},{10... | collective-permute-start | bytes 1572872 | tf_op jit(solution)/shard_map/ppermute | solution.py:102
  360.7 58.7 %collective-permute-start.67 = (bf16[256,512]{1,0:T(8,128)(2,1)S(1)}, bf16[256,512]{1,0:T(8,128)(2,1)S(1)}, u32[]{:S(2)}, u32[]{:S(2)}) collective-permute-start(bf16[256,512]{1,0:T(8,128)(2,1)S(1)} %copy-done.64), channel_id=1, source_target_pairs={{0,24},{8,0},{16,8},{24,16},{1,25},{9,1},{17,9},{25,17},{2,26},{10... | collective-permute-start | bytes 786440 | tf_op jit(solution)/shard_map/ppermute | solution.py:102
  360.7 58.7 %collective-permute-start.66 = (bf16[256,512]{1,0:T(8,128)(2,1)S(1)}, bf16[256,512]{1,0:T(8,128)(2,1)S(1)}, u32[]{:S(2)}, u32[]{:S(2)}) collective-permute-start(bf16[256,512]{1,0:T(8,128)(2,1)S(1)} %copy-done.63), channel_id=1, source_target_pairs={{0,16},{8,24},{16,0},{24,8},{1,17},{9,25},{17,1},{25,9},{2,18},{10... | collective-permute-start | bytes 786440 | tf_op jit(solution)/shard_map/ppermute | solution.py:102
  360.8 24.2 %collective-permute-start.61 = (bf16[256,2048]{1,0:T(8,128)(2,1)S(1)}, bf16[256,2048]{1,0:T(8,128)(2,1)S(1)}, u32[]{:S(2)}, u32[]{:S(2)}) collective-permute-start(bf16[256,2048]{1,0:T(8,128)(2,1)S(1)} %collective-permute-done.57), channel_id=1, source_target_pairs={{0,8},{8,16},{16,24},{1,9},{9,17},{17,25},{2,10},{10,18},{18,26},{... | collective-permute-start | bytes 3145736 | tf_op jit(solution)/shard_map/ppermute | solution.py:128
  364.8 31.5 %collective-permute-start.59 = (bf16[256,2048]{1,0:T(8,128)(2,1)S(1)}, bf16[256,2048]{1,0:T(8,128)(2,1)S(1)}, u32[]{:S(2)}, u32[]{:S(2)}) collective-permute-start(bf16[256,2048]{1,0:T(8,128)(2,1)S(1)} %collective-permute-done.58), channel_id=1, source_target_pairs={{8,0},{16,8},{24,16},{9,1},{17,9},{25,17},{10,2},{18,10},{26,18},{... | collective-permute-start | bytes 3145736 | tf_op jit(solution)/shard_map/ppermute | solution.py:129
  371.2 25.6 %collective-permute-start.54 = (bf16[256,768]{1,0:T(8,128)(2,1)S(1)}, bf16[256,768]{1,0:T(8,128)(2,1)S(1)}, u32[]{:S(2)}, u32[]{:S(2)}) collective-permute-start(bf16[256,768]{1,0:T(8,128)(2,1)S(1)} %convolution_convert_fusion.2), channel_id=1, source_target_pairs={{0,4},{4,0},{1,5},{5,1},{2,6},{6,2},{3,7},{7,3},{8,12},{12,8},{9,1... | collective-permute-start | bytes 1179656 | tf_op jit(solution)/shard_map/ppermute | solution.py:31
  385.1 34.4 %collective-permute-start.65 = (bf16[256,512]{1,0:T(8,128)(2,1)S(1)}, bf16[256,512]{1,0:T(8,128)(2,1)S(1)}, u32[]{:S(2)}, u32[]{:S(2)}) collective-permute-start(bf16[256,512]{1,0:T(8,128)(2,1)S(1)} %copy-done.62), channel_id=1, source_target_pairs={{0,8},{8,16},{16,24},{24,0},{1,9},{9,17},{17,25},{25,1},{2,10},{10... | collective-permute-start | bytes 786440 | tf_op jit(solution)/shard_map/ppermute | solution.py:102
  396.3 20.7 %collective-permute-start.72 = (bf16[1024,512]{1,0:T(8,128)(2,1)S(1)}, bf16[1024,512]{1,0:T(8,128)(2,1)S(1)}, u32[]{:S(2)}, u32[]{:S(2)}) collective-permute-start(bf16[1024,512]{1,0:T(8,128)(2,1)S(1)} %pad_maximum_fusion.10), channel_id=1, source_target_pairs={{0,1},{1,0},{2,3},{3,2},{4,5},{5,4},{6,7},{7,6},{8,9},{9,8},{10,11... | collective-permute-start | bytes 3145736 | tf_op jit(solution)/shard_map/ppermute | solution.py:31
  396.8 14.4 %collective-permute-start.55 = (bf16[1024,256]{1,0:T(8,128)(2,1)S(1)}, bf16[1024,256]{1,0:T(8,128)(2,1)S(1)}, u32[]{:S(2)}, u32[]{:S(2)}) collective-permute-start(bf16[1024,256]{1,0:T(8,128)(2,1)S(1)} %pad_maximum_fusion.16), channel_id=1, source_target_pairs={{0,2},{1,3},{2,0},{3,1},{4,6},{5,7},{6,4},{7,5},{8,10},{9,11},{10,... | collective-permute-start | bytes 1572872 | tf_op jit(solution)/shard_map/ppermute | solution.py:31
  411.2 27.9 %collective-permute-start.62 = (bf16[256,2048]{1,0:T(8,128)(2,1)S(1)}, bf16[256,2048]{1,0:T(8,128)(2,1)S(1)}, u32[]{:S(2)}, u32[]{:S(2)}) collective-permute-start(bf16[256,2048]{1,0:T(8,128)(2,1)S(1)} %collective-permute-done.61), channel_id=1, source_target_pairs={{0,8},{8,16},{16,24},{1,9},{9,17},{17,25},{2,10},{10,18},{18,26},{... | collective-permute-start | bytes 3145736 | tf_op jit(solution)/shard_map/ppermute | solution.py:128
  417.0 26.3 %collective-permute-start.60 = (bf16[256,2048]{1,0:T(8,128)(2,1)S(1)}, bf16[256,2048]{1,0:T(8,128)(2,1)S(1)}, u32[]{:S(2)}, u32[]{:S(2)}) collective-permute-start(bf16[256,2048]{1,0:T(8,128)(2,1)S(1)} %collective-permute-done.59), channel_id=1, source_target_pairs={{8,0},{16,8},{24,16},{9,1},{17,9},{25,17},{10,2},{18,10},{26,18},{... | collective-permute-start | bytes 3145736 | tf_op jit(solution)/shard_map/ppermute | solution.py:129
  419.4 28.3 %collective-permute-start.56 = (bf16[1024,512]{1,0:T(8,128)(2,1)S(1)}, bf16[1024,512]{1,0:T(8,128)(2,1)S(1)}, u32[]{:S(2)}, u32[]{:S(2)}) collective-permute-start(bf16[1024,512]{1,0:T(8,128)(2,1)S(1)} %pad_maximum_fusion.8), channel_id=1, source_target_pairs={{0,1},{1,0},{2,3},{3,2},{4,5},{5,4},{6,7},{7,6},{8,9},{9,8},{10,11... | collective-permute-start | bytes 3145736 | tf_op jit(solution)/shard_map/ppermute | solution.py:31
  444.6 15.1 %collective-permute-start.63 = (bf16[256,1024]{1,0:T(8,128)(2,1)S(1)}, bf16[256,1024]{1,0:T(8,128)(2,1)S(1)}, u32[]{:S(2)}, u32[]{:S(2)}) collective-permute-start(bf16[256,1024]{1,0:T(8,128)(2,1)S(1)} %convolution_convert_fusion.1), channel_id=1, source_target_pairs={{0,4},{4,0},{1,5},{5,1},{2,6},{6,2},{3,7},{7,3},{8,12},{12,8},{9,1... | collective-permute-start | bytes 1572872 | tf_op jit(solution)/shard_map/ppermute | solution.py:31
  447.6 21.1 %collective-permute-start.64 = (bf16[256,1024]{1,0:T(8,128)(2,1)S(1)}, bf16[256,1024]{1,0:T(8,128)(2,1)S(1)}, u32[]{:S(2)}, u32[]{:S(2)}) collective-permute-start(bf16[256,1024]{1,0:T(8,128)(2,1)S(1)} %convolution_convert_fusion), channel_id=1, source_target_pairs={{0,4},{4,0},{1,5},{5,1},{2,6},{6,2},{3,7},{7,3},{8,12},{12,8},{9,1... | collective-permute-start | bytes 1572872 | tf_op jit(solution)/shard_map/ppermute | solution.py:31
  (154 other events, 1458.1 us)
